TPU v7x, 256 devices: a whole 4x4x8 slice. The times are simulated.
256 devices in a mesh: section: 4 (over x), ctx: 32 (over z, y), tp: 2 (over core).
Axes of the slice: x: 4, y: 4, z: 8, core: 2. Of those that a mesh axis runs over, the one named last changes fastest.
Arguments:
- hidden: bfloat16 [4, 4096, 8192], P('section', 'ctx', 'tp')
- gain: bfloat16 [4, 8192], P('section', 'tp'), may hold values from 0.5 to 1.5
- queries: bfloat16 [4, 4096, 32, 128], P('section', 'ctx', 'tp')
- key_value_weight: bfloat16 [4, 8192, 4, 2, 128], P('section', 'ctx', 'tp')
- adapt_down: bfloat16 [4, 16, 4096], P('section', None, 'tp'), may hold values from -1 to 1
- adapt_up: bfloat16 [4, 16, 8192], P('section', None, 'tp'), may hold values from -0.75 to 0.75
- out_grad: bfloat16 [4, 4096, 8192], P('section', 'ctx', 'tp'), may hold values from -6 to 6
- doc_ids: int32 [4096], P('ctx'), may hold values from 0 to 63, never falling along the last dimension, each value on 1 to 3072 neighbouring positions
Outputs:
- attention_out: bfloat16 [4, 4096, 4096], P('section', 'ctx', 'tp')
- adapter_out: bfloat16 [4, 4096, 8192], P('section', 'ctx', 'tp')
- grad_down: float32 [4, 16, 4096], P('section', None, 'tp')
- grad_up: float32 [4, 16, 8192], P('section', None, 'tp')
Inputs may be any that keep to these rules, and one draw needn't show every extreme that they name: doc_ids never falls along the sequence; a document spans at most three quarters of 4096 tokens, and one spans exactly that.
All inputs are finite; a program needn't handle non-finite values.
Results may differ from a plain program's by a relative error of at most 0.022.
Values may be sent and summed in bfloat16 or wider, within the bound.
A program may use at most 128 MiB of HBM per device.

v0:
```python
import math

import jax
import jax.numpy as jnp
from jax import lax
from jax.sharding import PartitionSpec as P


def rotate(head_values, positions):
    half_width = head_values.shape[-1] // 2
    freqs = 1000000.0 ** (-jnp.arange(half_width, dtype=jnp.float32) * 2.0 / head_values.shape[-1])
    angles = positions.astype(jnp.float32)[:, None] * freqs[None, :]
    cosine = jnp.cos(angles)[:, None, :]
    sine_table = jnp.sin(angles)[:, None, :]
    first_half = head_values[..., :half_width]
    second_half = head_values[..., half_width:]
    return jnp.concatenate(
        [
            first_half * cosine - second_half * sine_table,
            second_half * cosine + first_half * sine_table,
        ],
        axis=-1,
    )


def per_device(hidden, gain, queries, key_value_weight, adapt_down, adapt_up, out_grad, doc_ids):
    tp_count = lax.axis_size("tp")
    row_count = hidden.shape[1]
    local_width = hidden.shape[2]
    head_dim = key_value_weight.shape[-1]
    kv_count = key_value_weight.shape[2]
    head_count = queries.shape[2]
    group_size = head_count // kv_count
    local_query = head_count * head_dim
    rank_size = adapt_down.shape[1]
    key_block = 1024
    full_rows, full_gain = (
        lax.all_gather(hidden, "tp", axis=2, tiled=True),
        lax.all_gather(gain, "tp", axis=1, tiled=True),
    )
    widened = full_rows[0].astype(jnp.float32)
    normalized_rows = (
        widened
        * lax.rsqrt(jnp.mean(widened * widened, axis=1, keepdims=True) + 1e-06)
        * full_gain[0].astype(jnp.float32)
    ).astype(jnp.bfloat16)
    kv_local = key_value_weight.reshape(1, key_value_weight.shape[1], kv_count * 2 * head_dim)
    keyval_raw = jnp.dot(
        normalized_rows,
        lax.all_gather(kv_local, "ctx", axis=1, tiled=True)[0],
        preferred_element_type=jnp.float32,
    )
    positions = lax.axis_index("ctx") * row_count + jnp.arange(row_count, dtype=jnp.int32)
    key_value_rows = keyval_raw.reshape(row_count, kv_count, 2, head_dim)
    rotated_keys = rotate(key_value_rows[:, :, 0], positions).astype(jnp.bfloat16)
    value_rows = key_value_rows[:, :, 1].astype(jnp.bfloat16)
    rotated_query = rotate(queries[0].astype(jnp.float32), positions).astype(jnp.bfloat16)
    stacked = (
        rotated_query.reshape(row_count, kv_count, group_size, head_dim)
        .transpose(1, 2, 0, 3)
        .reshape(kv_count, group_size * row_count, head_dim)
    )
    query_pos = jnp.tile(positions, group_size)
    query_doc = jnp.tile(doc_ids, group_size).astype(jnp.float32)
    score_scale = head_dim ** (-0.5)
    start_state = (
        jnp.full((kv_count, group_size * row_count), -1e30, jnp.float32),
        jnp.zeros((kv_count, group_size * row_count), jnp.float32),
        jnp.zeros((kv_count, group_size * row_count, head_dim), jnp.float32),
    )
    carried = start_state
    first_row = jnp.int32(0)
    piece_keys = lax.all_gather(rotated_keys, "ctx", axis=0, tiled=True)
    piece_values = lax.all_gather(value_rows, "ctx", axis=0, tiled=True)
    piece_docs = lax.all_gather(doc_ids.astype(jnp.bfloat16), "ctx", axis=0, tiled=True)
    key_total = piece_keys.shape[0]
    for block_start in range(0, key_total, key_block):
        block_stop = min(key_total, block_start + key_block)
        block_keys = piece_keys[block_start:block_stop]
        block_values = piece_values[block_start:block_stop]
        key_pos = first_row + block_start + jnp.arange(block_keys.shape[0], dtype=jnp.int32)
        key_doc = piece_docs[block_start:block_stop].astype(jnp.float32)
        running_top, running_sum, running_acc = carried
        scores = (
            jnp.einsum("gqd,kgd->gqk", stacked, block_keys, preferred_element_type=jnp.float32)
            * score_scale
        )
        allowed = (
            (key_pos[None, :] <= query_pos[:, None]) & (key_doc[None, :] == query_doc[:, None])
        )[None]
        scores = jnp.where(allowed, scores, -1e30)
        new_top = jnp.maximum(running_top, jnp.max(scores, axis=2))
        weights = jnp.where(allowed, jnp.exp(scores - new_top[:, :, None]), 0.0)
        shrink = jnp.exp(running_top - new_top)
        new_acc = running_acc * shrink[:, :, None] + jnp.einsum(
            "gqk,kgd->gqd",
            weights.astype(jnp.bfloat16),
            block_values,
            preferred_element_type=jnp.float32,
        )
        carried = (new_top, running_sum * shrink + jnp.sum(weights, axis=2), new_acc)
    final_top, final_sum, final_acc = carried
    attended = (
        (final_acc / final_sum[:, :, None])
        .reshape(kv_count, group_size, row_count, head_dim)
        .transpose(2, 0, 1, 3)
        .reshape(row_count, local_query)
        .astype(jnp.bfloat16)
    )
    low_part = jnp.dot(attended, adapt_down[0].T, preferred_element_type=jnp.float32)
    back_part = jnp.dot(out_grad[0], adapt_up[0].T, preferred_element_type=jnp.float32)
    low_sum, back_sum = lax.psum((low_part, back_part), "tp")
    low_rows = low_sum.astype(jnp.bfloat16)
    back_rows = back_sum.astype(jnp.bfloat16)
    adapter_rows = jnp.dot(low_rows, adapt_up[0], preferred_element_type=jnp.float32).astype(
        jnp.bfloat16
    )
    up_part = jnp.dot(low_rows.T, out_grad[0], preferred_element_type=jnp.float32)
    down_part = jnp.dot(back_rows.T, attended, preferred_element_type=jnp.float32)
    ceiling = 0.5 * math.sqrt(
        lax.axis_size("section") * rank_size * (local_query + local_width) * tp_count
    )
    up_total, down_total = (
        lax.psum(up_part.astype(jnp.bfloat16), "ctx").astype(jnp.float32),
        lax.psum(down_part.astype(jnp.bfloat16), "ctx").astype(jnp.float32),
    )
    local_squares = jnp.sum(up_total * up_total) + jnp.sum(down_total * down_total)
    squares = lax.psum(local_squares, ("section", "tp"))
    factor = jnp.minimum(1.0, ceiling / (jnp.sqrt(squares) + 1e-06))
    grad_up = up_total * factor
    grad_down = down_total * factor
    return (attended[None], adapter_rows[None], grad_down[None], grad_up[None])


def solution(mesh):
    return jax.shard_map(
        per_device,
        mesh=mesh,
        in_specs=(
            P("section", "ctx", "tp"),
            P("section", "tp"),
            P("section", "ctx", "tp", None),
            P("section", "ctx", "tp", None, None),
            P("section", None, "tp"),
            P("section", None, "tp"),
            P("section", "ctx", "tp"),
            P("ctx"),
        ),
        out_specs=(
            P("section", "ctx", "tp"),
            P("section", "ctx", "tp"),
            P("section", None, "tp"),
            P("section", None, "tp"),
        ),
        check_vma=False,
    )
```

profile of v0, /device:TPU:1, one launch (start us, length us, event | category | flops | bytes accessed | tf_op | source)
XLA Modules:
  0.0 494.9 jit_solution(17314606590005313898)
XLA Ops:
  8.0 1.9 copy.81
  9.9 4.9 all_gather.20
  15.1 15.2 %all-gather.7.cloned.1.call-done = bf16[1,128,8192]{2,1,0:T(8,128)(2,1)} async-done(((bf16[1,128,4096]{2,1,0:T(8,128)(2,1)}), bf16[1,128,8192]{2,1,0:T(8,128)(2,1)}) %all-gather.7.cloned.1.call-update) | async-done | bytes 2097168 | tf_op jit(solution)/shard_map/all_gather | solution.py:38
  30.3 2.1 fusion.13
  32.4 102.8 %all-gather.9.cloned.1.call-done = bf16[1,8192,512]{1,2,0:T(8,128)(2,1)} async-done(((bf16[1,256,512]{1,2,0:T(8,128)(2,1)}), bf16[1,8192,512]{1,2,0:T(8,128)(2,1)}) %all-gather.9.cloned.1.call-update) | async-done | bytes 8388624 | tf_op jit(solution)/shard_map/all_gather | solution.py:50
  135.1 6.4 %fusion.30 = f32[128,2,2,128]{0,3,2,1:T(8,128)S(1)} fusion(bf16[2,2,128,8192]{3,2,1,0:T(8,128)(2,1)} %bitcast.101, bf16[1,128,8192]{2,1,0:T(8,128)(2,1)} %all-gather.7.cloned.1.call-done, f32[8192]{0:T(1024)S(1)} %bitcast.96, f32[128]{0:T(128)S(1)} %add_rsqrt_fusion), kind=kOutput, calls=%fused_computation.43 | convolution fusion | flops 1077936128 | bytes 10781184 | tf_op jit(solution)/shard_map/dot_general | solution.py:48
  143.5 28.6 %all-gather.1 = bf16[32,1,128]{2,1,0:T(2,128)(2,1)S(1)} all-gather(bf16[1,1,128]{2,1,0:T(2,128)(2,1)S(1)} %get-tuple-element.39), channel_id=1, replica_groups=mesh['section'=4,'ctx'=32,'tp'=2] {'ctx'}, dimensions={0}, use_global_device_ids=true | all-gather | bytes 8448 | tf_op jit(solution)/shard_map/all_gather | solution.py:75
  173.7 4.4 fusion.24
  179.1 35.1 %all-gather.11.cloned.1.call-done = bf16[4096,2,128]{0,2,1:T(8,128)(2,1)} async-done(((bf16[128,2,128]{0,2,1:T(8,128)(2,1)}), bf16[4096,2,128]{0,2,1:T(8,128)(2,1)}) %all-gather.11.cloned.1.call-update) | async-done | bytes 2097168 | tf_op jit(solution)/shard_map/all_gather | solution.py:73
  214.2 3.3 fusion
  217.6 2.2 fusion.2
  219.8 5.8 %fusion.1 = (f32[2,1024]{1,0:T(2,128)S(1)}, f32[2,1024,1024]{1,2,0:T(8,128)}) fusion(pred[1024,1024]{0,1:T(8,128)(4,1)S(1)} %copy-done.9, bf16[2,1024,128]{2,1,0:T(8,128)(2,1)S(1)} %bitcast.93, bf16[4096,2,128]{0,2,1:T(8,128)(2,1)S(1)} %copy-done.15), kind=kOutput, calls=%fused_computation.9 | convolution fusion | flops 543160320 | bytes 10493952 | tf_op jit(solution)/shard_map/gqd,kgd->gqk/dot_general | solution.py:85
  225.6 2.2 fusion.3
  227.8 9.7 %fusion.4 = (f32[2,1024]{1,0:T(2,128)S(1)}, f32[2,1024]{1,0:T(2,128)S(1)}) fusion(f32[2,1024,1024]{1,2,0:T(8,128)S(1)} %get-tuple-element.48, f32[2,1024]{1,0:T(2,128)S(1)} %get-tuple-element.32, pred[1024,1024]{0,1:T(8,128)(4,1)S(1)} %get-tuple-element.33, f32[2,1024]{1,0:T(2,128)S(1)} %get-tuple-element.22, f32[2,1024,1024]{1,2,0:T(8,128)} %get-tuple-element.46, ...), kind=kLoop, calls=%fused_computation.12 | loop fusion | flops 20967424 | bytes 18907136 | tf_op jit(solution)/shard_map/reduce_sum | solution.py:101
  237.6 5.8 %fusion.8 = (f32[2,1024]{1,0:T(2,128)S(1)}, f32[2,1024]{1,0:T(2,128)S(1)}) fusion(f32[2,1024,1024]{1,2,0:T(8,128)S(1)} %get-tuple-element.44, f32[2,1024]{1,0:T(2,128)S(1)} %get-tuple-element.21, pred[1024,1024]{0,1:T(8,128)(4,1)} %get-tuple-element.35, f32[2,1024]{1,0:T(2,128)S(1)} %get-tuple-element.20, f32[2,1024,1024]{1,2,0:T(8,128)S(1)} %get-tuple-element.42, ...), kind=kLoop, calls=%fused_computation.16 | loop fusion | flops 20967424 | bytes 18907136 | tf_op jit(solution)/shard_map/reduce_sum | solution.py:101
  243.5 47.7 %all-gather.13.cloned.1.call-done = bf16[4096,2,1,128]{0,3,2,1:T(8,128)(2,1)} async-done(((bf16[128,2,1,128]{0,3,2,1:T(8,128)(2,1)}), bf16[4096,2,1,128]{0,3,2,1:T(8,128)(2,1)}) %all-gather.13.cloned.1.call-update) | async-done | bytes 2097168 | tf_op jit(solution)/shard_map/all_gather | solution.py:74
  291.2 7.9 %fusion.20 = f32[2,1024,128]{2,1,0:T(8,128)} fusion(f32[2,1024,1024]{1,2,0:T(8,128)} %get-tuple-element.46, f32[2,1024]{1,0:T(2,128)S(1)} %get-tuple-element.22, pred[1024,1024]{0,1:T(8,128)(4,1)S(1)} %copy-done.10, bf16[4096,2,1,128]{0,3,2,1:T(8,128)(2,1)} %all-gather.13.cloned.1.call-done), kind=kOutput, calls=%fused_computation.31 | convolution fusion | flops 547356672 | bytes 11018240 | tf_op jit(solution)/shard_map/gqk,kgd->gqd/dot_general | solution.py:95
  299.0 5.6 %fusion.18 = f32[2,1024,128]{2,1,0:T(8,128)} fusion(f32[2,1024,1024]{1,2,0:T(8,128)S(1)} %copy-done.3, f32[2,1024]{1,0:T(2,128)S(1)} %get-tuple-element.21, pred[1024,1024]{0,1:T(8,128)(4,1)} %get-tuple-element.35, bf16[4096,2,1,128]{0,3,2,1:T(8,128)(2,1)} %all-gather.13.cloned.1.call-done), kind=kOutput, calls=%fused_computation.30 | convolution fusion | flops 547356672 | bytes 11018240 | tf_op jit(solution)/shard_map/gqk,kgd->gqd/dot_general | solution.py:95
  304.7 4.9 fusion.16
  309.7 5.5 %divide_convert_fusion = bf16[2,1024,128]{2,1,0:T(8,128)(2,1)S(1)} fusion(f32[2,1024,128]{2,1,0:T(8,128)S(1)} %fusion.16, f32[2,1024,128]{2,1,0:T(8,128)S(1)} %copy-done.18, f32[2,1024,128]{2,1,0:T(8,128)S(1)} %copy-done.17, f32[2,1024,1024]{1,2,0:T(8,128)S(1)} %bitcast.84, f32[2,1024]{1,0:T(2,128)S(1)} %get-tuple-element.32, ...), kind=kOutput, calls=%fused_computation.56 | convolution fusion | flops 549715968 | bytes 13680640 | tf_op jit(solution)/shard_map/gqk,kgd->gqd/dot_general | solution.py:95
  315.7 6.8 %all-reduce = (bf16[128,16]{0,1:T(8,128)(2,1)S(1)}, bf16[128,16]{0,1:T(8,128)(2,1)S(1)}) all-reduce(f32[128,16]{0,1:T(8,128)S(1)} %fusion.76, f32[128,16]{0,1:T(8,128)S(1)} %fusion.56), channel_id=1, replica_groups=mesh['section'=4,'ctx'=32,'tp'=2] {'tp'}, use_global_device_ids=true, to_apply=%region_9.10 | all-reduce | flops 4096 | bytes 24576 | tf_op jit(solution)/shard_map/psum | solution.py:112
  325.8 135.9 %all-reduce.4.cloned.1.call-done = (bf16[16,2048]{1,0:T(8,128)(2,1)}, bf16[16,4096]{1,0:T(8,128)(2,1)}) async-done(((bf16[16,2048]{1,0:T(8,128)(2,1)}, bf16[16,4096]{1,0:T(8,128)(2,1)}), (bf16[16,2048]{1,0:T(8,128)(2,1)}, bf16[16,4096]{1,0:T(8,128)(2,1)})) %all-reduce.4.cloned.1.call-update) | async-done | bytes 196624 | tf_op jit(solution)/shard_map/psum | solution.py:125
  467.1 17.5 %psum.39 = f32[]{:T(128)} all-reduce(f32[]{:T(128)S(6)} %add.137), channel_id=1, replica_groups=mesh['section'=4,'ctx'=32,'tp'=2] {'section','tp'}, use_global_device_ids=true, to_apply=%region_15.16 | all-reduce | flops 1 | bytes 8 | tf_op jit(solution)/shard_map/psum | solution.py:128
  485.2 1.6 fusion.71
  (94 shorter events, 14.7 us)
Async XLA Ops:
  7.2 166.1 %copy-start = (bf16[1,128,4096]{2,1,0:T(8,128)(2,1)S(1)}, bf16[1,128,4096]{2,1,0:T(8,128)(2,1)}, u32[]{:S(2)}) copy-start(bf16[1,128,4096]{2,1,0:T(8,128)(2,1)} %param.14) | copy-start | bytes 3145732
  7.2 23.1 %all-gather.7.cloned.1.call-start = ((), (), s32[]{:S(2)}) async-start(), calls=%async_computation | async-start | bytes 3145728 | tf_op jit(solution)/shard_map/all_gather | solution.py:38
  7.9 134.6 %copy-start.11 = (bf16[1,128,16,128]{3,2,1,0:T(8,128)(2,1)S(1)}, bf16[1,128,16,128]{3,2,1,0:T(8,128)(2,1)}, u32[]{:S(2)}) copy-start(bf16[1,128,16,128]{3,2,1,0:T(8,128)(2,1)} %param.10) | copy-start | bytes 1572868
  7.9 127.2 %all-gather.9.cloned.1.call-start = ((), (), s32[]{:S(2)}) async-start(), calls=%async_computation.1 | async-start | bytes 8650752 | tf_op jit(solution)/shard_map/all_gather | solution.py:50
  9.9 204.3 %all-gather.11.cloned.1.call-start = ((), (), s32[]{:S(2)}) async-start(), calls=%async_computation.2 | async-start | bytes 2162688 | tf_op jit(solution)/shard_map/all_gather | solution.py:73
  135.1 8.3 %copy-start.16 = (s32[128]{0:T(128)S(1)}, s32[128]{0:T(128)}, u32[]{:S(2)}) copy-start(s32[128]{0:T(128)} %param.15) | copy-start | bytes 1540
  135.1 38.2 %copy-start.13 = (bf16[1,16,4096]{2,1,0:T(8,128)(2,1)S(1)}, bf16[1,16,4096]{2,1,0:T(8,128)(2,1)}, u32[]{:S(2)}) copy-start(bf16[1,16,4096]{2,1,0:T(8,128)(2,1)} %param.13) | copy-start | bytes 393220
  142.3 148.8 %all-gather.13.cloned.1.call-start = ((), (), s32[]{:S(2)}) async-start(), calls=%async_computation.3 | async-start | bytes 2162688 | tf_op jit(solution)/shard_map/all_gather | solution.py:74
  178.1 49.7 %copy-start.5 = (pred[1024,1024]{0,1:T(8,128)(4,1)}, pred[1024,1024]{0,1:T(8,128)(4,1)S(1)}, u32[]{:S(2)}) copy-start(pred[1024,1024]{0,1:T(8,128)(4,1)S(1)} %get-tuple-element.33) | copy-start | bytes 3145732
  178.1 59.5 %copy-start.7 = (pred[1024,1024]{0,1:T(8,128)(4,1)}, pred[1024,1024]{0,1:T(8,128)(4,1)S(1)}, u32[]{:S(2)}) copy-start(pred[1024,1024]{0,1:T(8,128)(4,1)S(1)} %get-tuple-element.36) | copy-start | bytes 3145732
  178.8 282.9 %all-reduce.4.cloned.1.call-start = ((), (), s32[]{:S(2)}) async-start(), calls=%async_computation.4 | async-start | bytes 393216 | tf_op jit(solution)/shard_map/psum | solution.py:125
  217.5 10.3 %copy-start.1 = (f32[2,1024,1024]{1,2,0:T(8,128)}, f32[2,1024,1024]{1,2,0:T(8,128)S(1)}, u32[]{:S(2)}) copy-start(f32[2,1024,1024]{1,2,0:T(8,128)S(1)} %get-tuple-element.48) | copy-start | bytes 25165828
  219.7 17.9 %copy-start.2 = (f32[2,1024,1024]{1,2,0:T(8,128)}, f32[2,1024,1024]{1,2,0:T(8,128)S(1)}, u32[]{:S(2)}) copy-start(f32[2,1024,1024]{1,2,0:T(8,128)S(1)} %get-tuple-element.44) | copy-start | bytes 25165828
  227.8 9.8 %copy-start.4 = (f32[2,1024,1024]{1,2,0:T(8,128)}, f32[2,1024,1024]{1,2,0:T(8,128)S(1)}, u32[]{:S(2)}) copy-start(f32[2,1024,1024]{1,2,0:T(8,128)S(1)} %get-tuple-element.42) | copy-start | bytes 25165828
  237.6 53.5 %copy-start.10 = (pred[1024,1024]{0,1:T(8,128)(4,1)S(1)}, pred[1024,1024]{0,1:T(8,128)(4,1)}, u32[]{:S(2)}) copy-start(pred[1024,1024]{0,1:T(8,128)(4,1)} %get-tuple-element.34) | copy-start | bytes 3145732
  291.2 7.9 %copy-start.3 = (f32[2,1024,1024]{1,2,0:T(8,128)S(1)}, f32[2,1024,1024]{1,2,0:T(8,128)}, u32[]{:S(2)}) copy-start(f32[2,1024,1024]{1,2,0:T(8,128)} %copy-done.2) | copy-start | bytes 25165828
  291.2 13.5 %slice-start.2 = ((s8[8388608]{0:T(1024)(128)(4,1)}), s8[4194304]{0:T(1024)(128)(4,1)S(1)}, s32[]{:S(2)}) async-start(s8[8388608]{0:T(1024)(128)(4,1)} %bitcast.85), calls=%async_computation.7 | async-start | bytes 8388608
  299.0 5.6 %slice-start.3 = ((s8[8388608]{0:T(1024)(128)(4,1)}), s8[4194304]{0:T(1024)(128)(4,1)S(1)}, s32[]{:S(2)}) async-start(s8[8388608]{0:T(1024)(128)(4,1)} %bitcast.85), calls=%async_computation.8 | async-start | bytes 8388608
  299.0 10.6 %slice-start = ((s8[8388608]{0:T(1024)(128)(4,1)}), s8[4194304]{0:T(1024)(128)(4,1)S(1)}, s32[]{:S(2)}) async-start(s8[8388608]{0:T(1024)(128)(4,1)} %bitcast.83), calls=%async_computation.5 | async-start | bytes 8388608
  304.7 5.0 %slice-start.1 = ((s8[8388608]{0:T(1024)(128)(4,1)}), s8[4194304]{0:T(1024)(128)(4,1)S(1)}, s32[]{:S(2)}) async-start(s8[8388608]{0:T(1024)(128)(4,1)} %bitcast.83), calls=%async_computation.6 | async-start | bytes 8388608
  304.7 5.0 %copy-start.6 = (pred[1024,1024]{0,1:T(8,128)(4,1)S(1)}, pred[1024,1024]{0,1:T(8,128)(4,1)}, u32[]{:S(2)}) copy-start(pred[1024,1024]{0,1:T(8,128)(4,1)} %copy-done.5) | copy-start | bytes 3145732
  304.7 5.0 %copy-start.17 = (f32[2,1024,128]{2,1,0:T(8,128)S(1)}, f32[2,1024,128]{2,1,0:T(8,128)}, u32[]{:S(2)}) copy-start(f32[2,1024,128]{2,1,0:T(8,128)} %fusion.20) | copy-start | bytes 3145732
  304.7 5.0 %copy-start.18 = (f32[2,1024,128]{2,1,0:T(8,128)S(1)}, f32[2,1024,128]{2,1,0:T(8,128)}, u32[]{:S(2)}) copy-start(f32[2,1024,128]{2,1,0:T(8,128)} %fusion.18) | copy-start | bytes 3145732
  309.7 5.8 %copy-start.14 = (bf16[1,16,2048]{2,1,0:T(8,128)(2,1)S(1)}, bf16[1,16,2048]{2,1,0:T(8,128)(2,1)}, u32[]{:S(2)}) copy-start(bf16[1,16,2048]{2,1,0:T(8,128)(2,1)} %param.12) | copy-start | bytes 196612
  (4 other events, 12.3 us)
Sparse Core Ops, SparseCore 0:
  9.8 20.4 all-gather.6
  33.3 101.7 all-gather.8
  142.4 71.7 all-gather.10
  217.1 74.0 all-gather.12
  324.5 137.1 all-reduce.3
where the time goes:
time: 495 us
  waiting for transfers between devices  337 us (68%)
  blocking collectives  57.8 us (12%)
  matrix products  47.6 us (10%)
  other arithmetic  31 us (6%)
  between operations  16.3 us (3%)
    psum x1, waiting for transfers between devices, per_device(): lax.psum(down_part.astype(jnp.bfloat16), 'ctx').astype(jnp.float32)  136 us
    all_gather x1, waiting for transfers between devices, per_device(): lax.all_gather(kv_local, 'ctx', axis=1, tiled=True)[0]  103 us
    all_gather x1, waiting for transfers between devices, per_device(): piece_values = lax.all_gather(value_rows, 'ctx', axis=0, tiled=True)  47.7 us
    all_gather x1, waiting for transfers between devices, per_device(): piece_keys = lax.all_gather(rotated_keys, 'ctx', axis=0, tiled=True)  35.1 us
    all_gather x1, blocking collectives, per_device(): lax.all_gather(doc_ids.astype(jnp.bfloat16), 'ctx', axis=0, tiled=True)  28.6 us
    dot_general x4, matrix products, per_device(): jnp.einsum('gqk,kgd->gqd', weights.astype(jnp.bfloat16), block_values, pr...  23.9 us
    psum x1, blocking collectives, per_device(): squares = lax.psum(local_squares, ('section', 'tp'))  17.5 us
    reduce_sum x2, other arithmetic, per_device(): jnp.sum(weights, axis=2)  15.6 us
  transfers between devices with their start and end apart: 5, of which 5 were waited for; matrix products, arithmetic and copies ran while one was open for 9% of the time, Pallas kernels for 0%

commit v1 on v0

v1 whole, which is shorter than its diff:
```python
import math

import jax
import jax.numpy as jnp
from jax import lax
from jax.experimental import pallas as pl
from jax.experimental.pallas import tpu as pltpu
from jax.sharding import PartitionSpec as P

MESH = pl.DeviceIdType.MESH
NY = 4
F32 = jnp.float32
BF16 = jnp.bfloat16


def remote(src, dst, send_sem, recv_sem, **where):
    return pltpu.make_async_remote_copy(
        src_ref=src,
        dst_ref=dst,
        send_sem=send_sem,
        recv_sem=recv_sem,
        device_id=where,
        device_id_type=MESH,
    )


def position():
    ctx = lax.axis_index("ctx")
    return ctx // NY, ctx % NY, lax.axis_index("tp")


class Ring:
    def __init__(self, nz, block, half, send, recv, sib_send=None, sib_recv=None):
        self.nz, self.steps = nz, nz // 2
        self.block, self.half = block, half
        self.send, self.recv = send, recv
        self.sib_send, self.sib_recv = sib_send, sib_recv
        self.z, self.y, self.t = position()

    def origin(self, d, s):
        return (self.z - s + self.nz) % self.nz if d == 0 else (self.z + s) % self.nz

    def neighbour(self, d):
        z = (self.z + 1) % self.nz if d == 0 else (self.z + self.nz - 1) % self.nz
        return dict(ctx=z * NY + self.y, tp=self.t)

    def piece(self, zi, d, s):
        return self.half(zi, d, self.t) if s == self.steps else self.block(zi, self.t)

    def hop(self, d, s, src=None):
        piece = self.piece(self.origin(d, s - 1), d, s)
        return remote(
            piece if src is None else src,
            piece,
            self.send.at[d, s - 1],
            self.recv.at[d, s - 1],
            **self.neighbour(d),
        )

    def arrival(self, d, s):
        piece = self.piece(self.origin(d, s), d, s)
        return remote(
            piece, piece, self.send.at[d, s - 1], self.recv.at[d, s - 1], **self.neighbour(d)
        )

    def aside(self, index, zi, core, src=None):
        piece = self.block(zi, core)
        return remote(
            piece if src is None else src,
            piece,
            self.sib_send.at[index],
            self.sib_recv.at[index],
            tp=1 - self.t,
        )

    def start(self, src=None):
        for d in (0, 1):
            self.hop(d, 1, src).start()
        if self.sib_send is not None:
            self.aside(0, self.z, self.t, src).start()

    def step(self, s):
        for d in (0, 1):
            self.arrival(d, s).wait_recv()
            self.hop(d, s + 1).start()
            if self.sib_send is not None:
                self.aside(2 * s - 1 + d, self.origin(d, s), self.t).start()

    def final(self):
        for d in (0, 1):
            self.arrival(d, self.steps).wait_recv()
        if self.sib_send is not None:
            self.aside(self.nz - 1, self.origin(0, self.steps), self.t).start()

    def asides(self):
        yield 0, self.z
        for s in range(1, self.steps):
            for d in (0, 1):
                yield 2 * s - 1 + d, self.origin(d, s)
        yield self.nz - 1, self.origin(0, self.steps)

    def wait_sibling(self):
        for index, zi in self.asides():
            self.aside(index, zi, 1 - self.t).wait_recv()

    def drain(self):
        for d in (0, 1):
            for s in range(1, self.steps + 1):
                self.hop(d, s).wait_send()
        if self.sib_send is not None:
            for index, zi in self.asides():
                self.aside(index, zi, self.t).wait_send()


def gather_kernel(
    nz,
    hid_ref,
    gain_ref,
    w_ref,
    q_ref,
    cos_ref,
    sin_ref,
    grad_ref,
    up_ref,
    down_ref,
    doc_ref,
    q_out,
    k_out,
    v_out,
    doc_out,
    back_out,
    down_out,
    w_buf,
    normed,
    x_buf,
    square_src,
    square_in,
    back_src,
    back_in,
    down_buf,
    doc_in,
    k_part,
    k_in,
    v_part,
    v_in,
    w_send,
    w_recv,
    ws_send,
    ws_recv,
    kv_send,
    kv_recv,
    kvs_send,
    kvs_recv,
    d_send,
    d_recv,
    x_send,
    x_recv,
    q_send,
    q_recv,
    rs_send,
    rs_recv,
    dy_send,
    dy_recv,
    pair_send,
    pair_recv,
):
    z, y, t = position()
    rows, width = hid_ref.shape
    depth = w_ref.shape[1]
    cols = depth * nz // 2
    head_dim = k_out.shape[-1]
    toks = 2 * rows
    home = y // 2

    barrier = pltpu.get_barrier_semaphore()
    for oz in (1, nz - 1):
        pl.semaphore_signal(
            barrier,
            inc=1,
            device_id=dict(ctx=(z + oz) % nz * NY + y, tp=t),
            device_id_type=MESH,
        )
    for oy in range(NY):
        for ot in range(2):
            if oy or ot:
                pl.semaphore_signal(
                    barrier,
                    inc=1,
                    device_id=dict(ctx=z * NY + (y + oy) % NY, tp=(t + ot) % 2),
                    device_id_type=MESH,
                )
    pl.semaphore_wait(barrier, 2 + 2 * NY - 1)

    def w_block(p):
        return lambda zi, core: w_buf.at[p, core, pl.ds(pl.multiple_of(zi * depth, depth), depth)]

    def w_half(p):
        return lambda zi, h, core: w_buf.at[
            p, core, pl.ds(pl.multiple_of(zi * depth + h * (depth // 2), depth // 2), depth // 2)
        ]

    def kv_half(buf):
        return lambda zi, h, core: buf.at[zi, core, pl.ds(h * (toks // 2), toks // 2)]

    w_rings = [
        Ring(nz, w_block(p), w_half(p), w_send.at[p], w_recv.at[p], ws_send.at[p], ws_recv.at[p])
        for p in (0, 1)
    ]
    kv_rings = [
        Ring(
            nz,
            lambda zi, core, buf=buf: buf.at[zi, core],
            kv_half(buf),
            kv_send.at[p],
            kv_recv.at[p],
            kvs_send.at[p],
            kvs_recv.at[p],
        )
        for p, buf in ((0, k_out), (1, v_out))
    ]

    w_rings[0].start(w_ref.at[0])
    sibling = dict(tp=1 - t)

    def doc_copy(oy):
        return remote(
            doc_ref,
            doc_in.at[oy - 1],
            dy_send.at[oy - 1],
            dy_recv.at[oy - 1],
            ctx=z * NY + (y + oy) % NY,
        )

    for oy in range(1, NY):
        doc_copy(oy).start()

    def down_copy(core):
        return remote(down_ref, down_buf.at[core], pair_send.at[0], pair_recv.at[0], **sibling)

    down_copy(t).start()

    hid = hid_ref[...].astype(F32)
    square = jnp.sum(hid * hid, axis=1, keepdims=True)
    square_src[...] = jnp.broadcast_to(square, square_src.shape)
    square_copy = remote(square_src, square_in, pair_send.at[1], pair_recv.at[1], **sibling)
    square_copy.start()
    down_buf[t] = down_ref[...]
    w_buf[0, t, pl.ds(pl.multiple_of(z * depth, depth), depth), :] = w_ref[0]
    w_buf[1, t, pl.ds(pl.multiple_of(z * depth, depth), depth), :] = w_ref[1]
    square_copy.wait_recv()
    mean = (square_src[:, :1] + square_in[:, :1]) * (1.0 / (2 * width))
    scale = lax.rsqrt(mean + 1e-06)

    def x_dest(b, core):
        return x_buf.at[pl.ds(b * rows, rows), pl.ds(pl.multiple_of(core * cols, cols), cols)]

    def x_copy(oy):
        yd = (y + oy) % NY
        return remote(
            normed.at[yd],
            x_dest(y % 2, t),
            x_send.at[oy],
            x_recv.at[y % 2, t],
            ctx=z * NY + yd,
            tp=home,
        )

    for yd in range(NY):
        for zl in range(nz // 2):
            start = (zl * NY + yd) * depth
            piece = hid_ref[:, start : start + depth].astype(F32)
            gain = gain_ref[:, start : start + depth].astype(F32)
            normed[yd, :, zl * depth : (zl + 1) * depth] = (piece * scale * gain).astype(BF16)
    for oy in range(1, NY):
        x_copy(oy).start()

    @pl.when(t != home)
    def _():
        x_copy(0).start()

    @pl.when(t == home)
    def _():
        x_buf[
            pl.ds(pl.multiple_of((y % 2) * rows, rows), rows),
            pl.ds(pl.multiple_of(t * cols, cols), cols),
        ] = normed[y]

    back_src[...] = lax.dot_general(
        up_ref[...], grad_ref[...], (((1,), (1,)), ((), ())), preferred_element_type=F32
    )
    back_copy = remote(back_src, back_in, pair_send.at[2], pair_recv.at[2], **sibling)
    back_copy.start()

    steps = nz // 2
    for s in range(1, steps):
        w_rings[0].step(s)
    w_rings[1].start(w_ref.at[1])
    w_rings[0].final()

    back_copy.wait_recv()
    back_out[...] = (back_src[...] + back_in[...]).astype(BF16)
    down_copy(1 - t).wait_recv()
    down_out[...] = down_buf[
        home, :, pl.ds(pl.multiple_of((y % 2) * down_out.shape[1], 128), down_out.shape[1])
    ]

    for oy in range(1, NY):
        doc_copy(oy).wait_recv()
    line = lax.broadcasted_iota(jnp.int32, doc_ref.shape, 0)
    group = jnp.where(line == y, doc_ref[...], 0)
    for oy in range(1, NY):
        group = jnp.where(line == (y + NY - oy) % NY, doc_in[oy - 1], group)
    doc_out[z] = group

    def doc_pass(d, s):
        zi = (z - s + 1 + nz) % nz if d == 0 else (z + s - 1) % nz
        to = (z + 1) % nz if d == 0 else (z + nz - 1) % nz
        return remote(
            doc_out.at[zi], doc_out.at[zi], d_send.at[d, s - 1], d_recv.at[d, s - 1], ctx=to * NY + y
        )

    def doc_arrive(d, s):
        zi = (z - s + nz) % nz if d == 0 else (z + s) % nz
        to = (z + 1) % nz if d == 0 else (z + nz - 1) % nz
        return remote(
            doc_out.at[zi], doc_out.at[zi], d_send.at[d, s - 1], d_recv.at[d, s - 1], ctx=to * NY + y
        )

    doc_hops = [(0, s) for s in range(1, steps + 1)] + [(1, s) for s in range(1, steps)]

    def doc_step(s):
        for d in (0, 1):
            if (d, s) in doc_hops:
                doc_arrive(d, s).wait_recv()
                if (d, s + 1) in doc_hops:
                    doc_pass(d, s + 1).start()

    for d in (0, 1):
        if (d, 1) in doc_hops:
            doc_pass(d, 1).start()

    if steps > 1:
        w_rings[1].step(1)

    def x_wait():
        for b in range(2):
            for core in range(2):
                src_y = 2 * t + b

                @pl.when(jnp.logical_or(src_y != y, t != core))
                def _():
                    dest = x_dest(b, core)
                    remote(
                        dest, dest, x_send.at[0], x_recv.at[b, core], **sibling
                    ).wait_recv()

    def project(p, part):
        for core in range(2):
            partial = jnp.dot(x_buf[...], w_buf[p, core], preferred_element_type=F32)
            for hl in range(2):
                part[2 * core + hl] = partial[:, hl * head_dim : (hl + 1) * head_dim].astype(part.dtype)

    def scatter_copy(p, oy):
        part, into = ((k_part, k_in), (v_part, v_in))[p]
        yd = (y + oy) % NY
        return remote(
            part.at[yd],
            into.at[oy - 1],
            rs_send.at[p, oy - 1],
            rs_recv.at[p, oy - 1],
            ctx=z * NY + yd,
        )

    def collect(p):
        part, into = ((k_part, k_in), (v_part, v_in))[p]
        for oy in range(1, NY):
            scatter_copy(p, oy).wait_recv()
        total = part[y].astype(F32)
        for oy in range(1, NY):
            total = total + into[oy - 1].astype(F32)
        return total

    x_wait()
    w_rings[0].wait_sibling()
    project(0, k_part)
    for oy in range(1, NY):
        scatter_copy(0, oy).start()
    for s in range(2, steps):
        w_rings[1].step(s)
        doc_step(s - 1)
    w_rings[1].final()
    w_rings[1].wait_sibling()
    project(1, v_part)
    for oy in range(1, NY):
        scatter_copy(1, oy).start()

    def q_dest(b):
        return q_out.at[:, pl.ds(b * rows, rows)]

    def q_copy(kvl):
        return remote(
            q_ref.at[kvl],
            q_dest(y % 2),
            q_send.at[kvl],
            q_recv.at[y % 2],
            ctx=z * NY + 2 * t + kvl,
            tp=home,
        )

    for kvl in range(2):
        own = jnp.logical_and(2 * t + kvl == y, home == t)

        @pl.when(jnp.logical_not(own))
        def _():
            q_copy(kvl).start()

        @pl.when(own)
        def _():
            q_out[:, pl.ds(pl.multiple_of((y % 2) * rows, rows), rows), :] = q_ref[kvl]

    keys = collect(0)
    k_out[z, t] = (keys * cos_ref[...] + pltpu.roll(keys, head_dim // 2, 1) * sin_ref[...]).astype(BF16)
    kv_rings[0].start()
    v_out[z, t] = collect(1).astype(BF16)
    kv_rings[1].start()
    for s in range(1, steps):
        kv_rings[0].step(s)
        kv_rings[1].step(s)
    kv_rings[0].final()
    kv_rings[1].final()
    for s in range(max(1, steps - 1), steps + 1):
        doc_step(s)
    kv_rings[0].wait_sibling()
    kv_rings[1].wait_sibling()

    for b in range(2):

        @pl.when(jnp.logical_or(2 * t + b != y, home != t))
        def _():
            dest = q_dest(b)
            remote(dest, dest, q_send.at[0], q_recv.at[b], **sibling).wait_recv()

    for ring in w_rings + kv_rings:
        ring.drain()
    for oy in range(1, NY):
        doc_copy(oy).wait_send()
        x_copy(oy).wait_send()
        scatter_copy(0, oy).wait_send()
        scatter_copy(1, oy).wait_send()

    @pl.when(t != home)
    def _():
        x_copy(0).wait_send()

    for kvl in range(2):

        @pl.when(jnp.logical_not(jnp.logical_and(2 * t + kvl == y, home == t)))
        def _():
            q_copy(kvl).wait_send()

    for d, s in doc_hops:
        doc_pass(d, s).wait_send()
    down_copy(t).wait_send()
    square_copy.wait_send()
    back_copy.wait_send()


def attend_kernel(q_ref, k_ref, v_ref, doc_ref, doc_smem, down_ref, out_ref, low_ref, top, total, acc):
    z, y, t = position()
    heads, toks, head_dim = q_ref.shape
    rows = toks // 2
    keys = k_ref.shape[1]
    factor = head_dim ** (-0.5) * math.log2(math.e)

    turned = jnp.transpose(doc_ref[z].astype(F32))
    lane = lax.broadcasted_iota(jnp.int32, turned.shape, 1)
    q_doc = jnp.concatenate(
        [
            jnp.sum(jnp.where(lane == 2 * t + b, turned, 0.0), axis=1, keepdims=True)
            for b in range(2)
        ],
        axis=0,
    )
    q_pos = t * toks + lax.broadcasted_iota(jnp.int32, (toks, keys), 0)
    k_pos = lax.broadcasted_iota(jnp.int32, (toks, keys), 1)
    first_doc = doc_smem[z, 2 * t, 0]

    def block(kb, first):
        k_doc = jnp.concatenate([doc_ref[kb, b : b + 1, :] for b in range(NY)], axis=1).astype(F32)
        allowed = k_doc == q_doc
        if first:
            allowed = jnp.logical_and(allowed, k_pos <= q_pos)
        bias = jnp.where(allowed, 0.0, -1e30)
        k = k_ref[kb]
        v = v_ref[kb]
        for h in range(heads):
            scores = (
                lax.dot_general(q_ref[h], k, (((1,), (1,)), ((), ())), preferred_element_type=F32)
                + bias
            )
            peak = jnp.max(scores, axis=1, keepdims=True)
            if first:
                new_top = peak
            else:
                old_top = top[h]
                new_top = jnp.maximum(old_top, peak)
                shrink = jnp.exp2((old_top - new_top) * factor)
            weights = jnp.exp2((scores - new_top) * factor)
            part_sum = jnp.sum(weights, axis=1, keepdims=True)
            part = jnp.dot(weights.astype(BF16), v, preferred_element_type=F32)
            top[h] = new_top
            if first:
                total[h] = part_sum
                acc[h] = part
            else:
                total[h] = total[h] * shrink + part_sum
                acc[h] = acc[h] * shrink + part

    block(z, True)

    def body(i, carry):
        kb = z - 1 - i

        @pl.when(doc_smem[kb, NY - 1, rows - 1] >= first_doc)
        def _():
            block(kb, False)

        return carry

    lax.fori_loop(0, z, body, 0)
    for h in range(heads):
        out_ref[:, h * head_dim : (h + 1) * head_dim] = (acc[h] / total[h]).astype(BF16)
    low_ref[...] = lax.dot_general(
        down_ref[...], out_ref[...], (((1,), (1,)), ((), ())), preferred_element_type=F32
    )


def adapt_kernel(
    nz,
    ceiling,
    sections,
    att_ref,
    low_ref,
    grad_ref,
    up_ref,
    back_ref,
    att_out,
    adapter_out,
    gdown_out,
    gup_out,
    low_src,
    low_in,
    red_src,
    red_in,
    all_buf,
    sq_src,
    sq_in,
    att_send,
    att_recv,
    low_send,
    low_recv,
    red_send,
    red_recv,
    all_send,
    all_recv,
    sq_send,
    sq_recv,
):
    z, y, t = position()
    section = lax.axis_index("section")
    count = nz * NY
    me = z * NY + y
    home = y // 2
    rows = att_out.shape[0]
    half_cols = att_ref.shape[1]
    rank = up_ref.shape[0]

    barrier = pltpu.get_barrier_semaphore()

    def greet(o, carry):
        pl.semaphore_signal(
            barrier, inc=1, device_id=dict(ctx=(me + o) % count, tp=t), device_id_type=MESH
        )
        return carry

    lax.fori_loop(1, count, greet, 0)
    for oy in range(NY):
        pl.semaphore_signal(
            barrier,
            inc=1,
            device_id=dict(ctx=z * NY + (y + oy) % NY, tp=1 - t),
            device_id_type=MESH,
        )
    for osec in range(1, sections):
        for ot in range(2):
            pl.semaphore_signal(
                barrier,
                inc=1,
                device_id=dict(section=(section + osec) % sections, tp=(t + ot) % 2),
                device_id_type=MESH,
            )
    pl.semaphore_wait(barrier, count - 1 + NY + 2 * (sections - 1))

    def low_copy(b, core):
        return remote(
            low_src.at[b],
            low_in.at[y],
            low_send.at[b, core],
            low_recv.at[y],
            ctx=z * NY + 2 * t + b,
            tp=core,
        )

    def low_own(b, core):
        return jnp.logical_and(2 * t + b == y, t == core)

    for b in range(2):
        low_src[b] = low_ref[:, b * rows : (b + 1) * rows]
    for b in range(2):
        for core in range(2):

            @pl.when(jnp.logical_not(low_own(b, core)))
            def _():
                low_copy(b, core).start()

            @pl.when(low_own(b, core))
            def _():
                low_in[y] = low_src[b]

    def att_dest(kvl):
        return att_out.at[:, pl.ds(pl.multiple_of(kvl * half_cols, half_cols), half_cols)]

    def att_copy(b):
        return remote(
            att_ref.at[pl.ds(b * rows, rows)],
            att_dest(y % 2),
            att_send.at[b],
            att_recv.at[y % 2],
            ctx=z * NY + 2 * t + b,
            tp=home,
        )

    def att_own(b):
        return jnp.logical_and(2 * t + b == y, home == t)

    for b in range(2):

        @pl.when(jnp.logical_not(att_own(b)))
        def _():
            att_copy(b).start()

        @pl.when(att_own(b))
        def _():
            att_out[:, pl.ds(pl.multiple_of((y % 2) * half_cols, half_cols), half_cols)] = att_ref[
                b * rows : (b + 1) * rows
            ]

    for src_y in range(NY):

        @pl.when(jnp.logical_or(src_y != y, home != t))
        def _():
            remote(
                low_in.at[src_y], low_in.at[src_y], low_send.at[0, 0], low_recv.at[src_y], tp=1 - t
            ).wait_recv()

    low = low_in[0]
    for src_y in range(1, NY):
        low = low + low_in[src_y]
    low = low.astype(BF16)

    for c in range(count):
        red_src[c, 0:rank, :] = jnp.dot(
            low, grad_ref[:, c * 128 : (c + 1) * 128], preferred_element_type=F32
        ).astype(BF16)

    for kvl in range(2):

        @pl.when(jnp.logical_or(2 * t + kvl != y, home != t))
        def _():
            dest = att_dest(kvl)
            remote(dest, dest, att_send.at[0], att_recv.at[kvl], tp=1 - t).wait_recv()

    down = jnp.dot(back_ref[...], att_out[...], preferred_element_type=F32)
    blocks = count // 2
    pad = jnp.zeros((8, 128), F32)
    for c in range(count):
        r0 = 8 * (c // blocks)
        c0 = 128 * (c % blocks)
        red_src[c, rank : rank + 16, :] = jnp.concatenate(
            [down[r0 : r0 + 8, c0 : c0 + 128], pad], axis=0
        ).astype(BF16)

    def red_copy(o):
        to = (me + o) % count
        return remote(
            red_src.at[to], red_in.at[o - 1], red_send.at[o - 1], red_recv.at[o - 1], ctx=to
        )

    def red_start(o, carry):
        red_copy(o).start()
        return carry

    lax.fori_loop(1, count, red_start, 0)

    adapter_out[...] = lax.dot_general(
        low, up_ref[...], (((0,), (0,)), ((), ())), preferred_element_type=F32
    ).astype(BF16)

    def red_add(o, sum_so_far):
        red_copy(o).wait_recv()
        return sum_so_far + red_in[o - 1].astype(F32)

    summed = lax.fori_loop(1, count, red_add, red_src[me].astype(F32))
    square = jnp.sum(jnp.sum(summed * summed, axis=1, keepdims=True), axis=0, keepdims=True)
    sq_src[...] = jnp.broadcast_to(square, sq_src.shape)

    peers = [(osec, ot) for osec in range(sections) for ot in range(2) if osec or ot]

    def sq_copy(i):
        osec, ot = peers[i]
        return remote(
            sq_src,
            sq_in.at[i],
            sq_send.at[i],
            sq_recv.at[i],
            section=(section + osec) % sections,
            tp=(t + ot) % 2,
        )

    for i in range(len(peers)):
        sq_copy(i).start()
    squares = sq_src[...]
    for i in range(len(peers)):
        sq_copy(i).wait_recv()
        squares = squares + sq_in[i]
    high = squares.astype(BF16)
    rest = (squares - high.astype(F32)).astype(BF16)
    line = lax.broadcasted_iota(jnp.int32, (8, 128), 0)
    tail = jnp.where(line < 4, high.astype(F32), rest.astype(F32))
    all_buf[me] = jnp.concatenate([summed[: rank + 8], tail], axis=0).astype(BF16)

    def all_copy(o):
        to = (me + o) % count
        return remote(all_buf.at[me], all_buf.at[me], all_send.at[o - 1], all_recv.at[o - 1], ctx=to)

    def all_arrive(o):
        of = (me - o + count) % count
        return remote(all_buf.at[of], all_buf.at[of], all_send.at[o - 1], all_recv.at[o - 1], ctx=of)

    def all_start(o, carry):
        all_copy(o).start()
        return carry

    lax.fori_loop(1, count, all_start, 0)

    def all_wait(o, carry):
        all_arrive(o).wait_recv()
        return carry

    lax.fori_loop(1, count, all_wait, 0)
    norm = jnp.zeros((8, 128), F32)
    for c in range(count):
        norm = norm + all_buf[c, rank : rank + 16, :].astype(F32)[8:]
    total = norm[0:1, 0:1] + norm[4:5, 0:1]
    clip = jnp.minimum(1.0, ceiling / (jnp.sqrt(total) + 1e-06))
    for c in range(count):
        r0 = 8 * (c // blocks)
        c0 = 128 * (c % blocks)
        gup_out[:, c * 128 : (c + 1) * 128] = all_buf[c, 0:rank, :].astype(F32) * clip
        gdown_out[r0 : r0 + 8, c0 : c0 + 128] = (
            all_buf[c, rank : rank + 16, :].astype(F32)[:8] * clip
        )

    def drain(o, carry):
        red_copy(o).wait_send()
        all_copy(o).wait_send()
        return carry

    lax.fori_loop(1, count, drain, 0)
    for i in range(len(peers)):
        sq_copy(i).wait_send()
    for b in range(2):

        @pl.when(jnp.logical_not(att_own(b)))
        def _():
            att_copy(b).wait_send()

        for core in range(2):

            @pl.when(jnp.logical_not(low_own(b, core)))
            def _():
                low_copy(b, core).wait_send()


def rope_tables(positions, head_dim):
    freqs = 1000000.0 ** (-jnp.arange(head_dim // 2, dtype=F32) * 2.0 / head_dim)
    angles = positions.astype(F32)[:, None] * freqs[None, :]
    cosine, sine = jnp.cos(angles), jnp.sin(angles)
    return jnp.concatenate([cosine, cosine], axis=1), jnp.concatenate([-sine, sine], axis=1)


def per_device(hidden, gain, queries, key_value_weight, adapt_down, adapt_up, out_grad, doc_ids):
    nz = lax.axis_size("ctx") // NY
    sections = lax.axis_size("section")
    rows, width = hidden.shape[1:]
    depth, kv_count = key_value_weight.shape[1:3]
    head_dim = key_value_weight.shape[-1]
    heads = queries.shape[2]
    group = heads // kv_count
    rank, local_query = adapt_down.shape[1:]
    toks = 2 * rows
    z, y, t = position()

    start = (z * 2 + t) * toks
    home_start = (z * NY + y) * rows
    cos_k, sin_k = rope_tables(start + jnp.arange(toks, dtype=jnp.int32), head_dim)
    cos_q, sin_q = rope_tables(home_start + jnp.arange(rows, dtype=jnp.int32), head_dim)
    q = queries[0].astype(F32)
    turned = jnp.concatenate([q[..., head_dim // 2 :], q[..., : head_dim // 2]], axis=-1)
    q = (q * cos_q[:, None, :] + turned * sin_q[:, None, :]).astype(BF16)
    q = q.reshape(rows, kv_count, group, head_dim).transpose(1, 2, 0, 3)
    w = key_value_weight[0].transpose(2, 0, 1, 3).reshape(2, depth, kv_count * head_dim)
    docs = jnp.broadcast_to(doc_ids[None, :], (8, rows))

    vmem = pl.BlockSpec(memory_space=pltpu.VMEM)
    smem = pl.BlockSpec(memory_space=pltpu.SMEM)
    dma = pltpu.SemaphoreType.DMA
    steps = nz // 2
    v_type = BF16
    q_all, k_all, v_all, doc_all, back, down = pl.pallas_call(
        lambda *refs: gather_kernel(nz, *refs),
        out_shape=(
            jax.ShapeDtypeStruct((group, toks, head_dim), BF16),
            jax.ShapeDtypeStruct((nz, 2, toks, head_dim), BF16),
            jax.ShapeDtypeStruct((nz, 2, toks, head_dim), BF16),
            jax.ShapeDtypeStruct((nz, 8, rows), jnp.int32),
            jax.ShapeDtypeStruct((rank, rows), BF16),
            jax.ShapeDtypeStruct((rank, local_query // 2), BF16),
        ),
        in_specs=[vmem] * 10,
        out_specs=[vmem] * 6,
        scratch_shapes=[
            pltpu.VMEM((2, 2, nz * depth, kv_count * head_dim), BF16),
            pltpu.VMEM((NY, rows, depth * nz // 2), BF16),
            pltpu.VMEM((toks, depth * nz), BF16),
            pltpu.VMEM((rows, 128), F32),
            pltpu.VMEM((rows, 128), F32),
            pltpu.VMEM((rank, rows), F32),
            pltpu.VMEM((rank, rows), F32),
            pltpu.VMEM((2, rank, local_query), BF16),
            pltpu.VMEM((NY - 1, 8, rows), jnp.int32),
            pltpu.VMEM((NY, toks, head_dim), F32),
            pltpu.VMEM((NY - 1, toks, head_dim), F32),
            pltpu.VMEM((NY, toks, head_dim), v_type),
            pltpu.VMEM((NY - 1, toks, head_dim), v_type),
            dma((2, 2, steps)),
            dma((2, 2, steps)),
            dma((2, nz)),
            dma((2, nz)),
            dma((2, 2, steps)),
            dma((2, 2, steps)),
            dma((2, nz)),
            dma((2, nz)),
            dma((2, steps)),
            dma((2, steps)),
            dma((NY,)),
            dma((2, 2)),
            dma((2,)),
            dma((2,)),
            dma((2, NY - 1)),
            dma((2, NY - 1)),
            dma((NY - 1,)),
            dma((NY - 1,)),
            dma((3,)),
            dma((3,)),
        ],
        compiler_params=pltpu.CompilerParams(collective_id=0, has_side_effects=True),
        name="gather",
    )(hidden[0], gain, w, q, cos_k, sin_k, out_grad[0], adapt_up[0], adapt_down[0], docs)

    keys = NY * rows
    attended, low = pl.pallas_call(
        attend_kernel,
        out_shape=(
            jax.ShapeDtypeStruct((toks, group * head_dim), BF16),
            jax.ShapeDtypeStruct((rank, toks), F32),
        ),
        in_specs=[vmem, vmem, vmem, vmem, smem, vmem],
        out_specs=[vmem, vmem],
        scratch_shapes=[
            pltpu.VMEM((group, toks, 1), F32),
            pltpu.VMEM((group, toks, 1), F32),
            pltpu.VMEM((group, toks, head_dim), F32),
        ],
        name="attend",
    )(
        q_all,
        k_all.reshape(nz, keys, head_dim),
        v_all.reshape(nz, keys, head_dim),
        doc_all,
        doc_all,
        down,
    )

    count = nz * NY
    chunk = rank + 16
    ceiling = 0.5 * math.sqrt(sections * rank * (local_query + width) * 2)
    peers = 2 * sections - 1
    return pl.pallas_call(
        lambda *refs: adapt_kernel(nz, ceiling, sections, *refs),
        out_shape=(
            jax.ShapeDtypeStruct((rows, local_query), BF16),
            jax.ShapeDtypeStruct((rows, width), BF16),
            jax.ShapeDtypeStruct((rank, local_query), F32),
            jax.ShapeDtypeStruct((rank, width), F32),
        ),
        in_specs=[vmem] * 5,
        out_specs=[vmem] * 4,
        scratch_shapes=[
            pltpu.VMEM((2, rank, rows), F32),
            pltpu.VMEM((NY, rank, rows), F32),
            pltpu.VMEM((count, chunk, 128), BF16),
            pltpu.VMEM((count - 1, chunk, 128), BF16),
            pltpu.VMEM((count, chunk, 128), BF16),
            pltpu.VMEM((8, 128), F32),
            pltpu.VMEM((peers, 8, 128), F32),
            dma((2,)),
            dma((2,)),
            dma((2, 2)),
            dma((NY,)),
            dma((count - 1,)),
            dma((count - 1,)),
            dma((count - 1,)),
            dma((count - 1,)),
            dma((peers,)),
            dma((peers,)),
        ],
        compiler_params=pltpu.CompilerParams(collective_id=1, has_side_effects=True),
        name="adapt",
    )(attended, low, out_grad[0], adapt_up[0], back)


def solution(mesh):
    def step(*args):
        return tuple(out[None] for out in per_device(*args))

    return jax.shard_map(
        step,
        mesh=mesh,
        in_specs=(
            P("section", "ctx", "tp"),
            P("section", "tp"),
            P("section", "ctx", "tp", None),
            P("section", "ctx", "tp", None, None),
            P("section", None, "tp"),
            P("section", None, "tp"),
            P("section", "ctx", "tp"),
            P("ctx"),
        ),
        out_specs=(
            P("section", "ctx", "tp"),
            P("section", "ctx", "tp"),
            P("section", None, "tp"),
            P("section", None, "tp"),
        ),
        check_vma=False,
    )
```

time: 495 us -> 149 us (0.30)
  waiting for transfers between devices: 337 us -> 0 us
  Pallas kernels: 0 us -> 136 us
  blocking collectives: 57.8 us -> 0 us
  matrix products: 47.6 us -> 0 us
  other arithmetic: 31 us -> 3.03 us
  between operations: 16.3 us -> 0.78 us
    all_gather x4 -> x0, waiting for transfers between devices: 201 us -> none  [the longest x1 103 us: per_device(): lax.all_gather(kv_local, 'ctx', axis=1, tiled=True)[0]]
    pallas_call x0 -> x3, Pallas kernels: none -> 136 us  [the longest x1 68.6 us: per_device(): pl.pallas_call(lambda *refs: gather_kernel(nz, *refs), out_shape=(jax.Sha...]
    psum x1 -> x0, waiting for transfers between devices: 136 us -> none  [per_device(): lax.psum(down_part.astype(jnp.bfloat16), 'ctx').astype(jnp.float32)]
    dot_general x14 -> x0, matrix products: 47.6 us -> none  [the longest x4 23.9 us: per_device(): jnp.einsum('gqk,kgd->gqd', weights.astype(jnp.bfloat16), block_values, pr...]
    all_gather x2 -> x0, blocking collectives: 33.6 us -> none  [the longest x1 28.6 us: per_device(): lax.all_gather(doc_ids.astype(jnp.bfloat16), 'ctx', axis=0, tiled=True)]
    psum x2 -> x0, blocking collectives: 24.2 us -> none  [the longest x1 17.5 us: per_device(): squares = lax.psum(local_squares, ('section', 'tp'))]
    reduce_sum x5 -> x0, other arithmetic: 20.7 us -> none  [the longest x2 15.6 us: per_device(): jnp.sum(weights, axis=2)]
  transfers between devices with their start and end apart: 5 -> 0, of which waited for: 5 -> 0; matrix products, arithmetic and copies ran while one was open for 9% -> 0% of each run, Pallas kernels for 0% -> 0%
where the time goes in v1:
time: 149 us; the launch traced here: 148 us
  Pallas kernels  136 us (91%)
  local copies, waits for them, and re-layouts  8.1 us (5%)
  other arithmetic  3.03 us (2%)
    pallas_call x1, Pallas kernels, per_device(): pl.pallas_call(lambda *refs: gather_kernel(nz, *refs), out_shape=(jax.Sha...  68.6 us
    pallas_call x1, Pallas kernels, per_device(): pl.pallas_call(lambda *refs: adapt_kernel(nz, ceiling, sections, *refs),...  62.1 us
    pallas_call x1, Pallas kernels, per_device(): pl.pallas_call(attend_kernel, out_shape=(jax.ShapeDtypeStruct((toks, grou...  5.8 us
    unnamed x16, local copies, waits for them, and re-layouts  5.36 us

profile of v1, /device:TPU:1, one launch (start us, length us, event | category | flops | bytes accessed | tf_op | source)
XLA Modules:
  0.0 148.4 jit_solution(16918539551404390084)
XLA Ops:
  0.7 0.3 multiply_cosine_fusion.1
  1.0 0.1 pad_maximum_fusion.2
  1.1 0.6 copy-done
  1.7 0.1 convert_bitcast_fusion
  1.8 0.3 fusion.5
  2.1 0.3 copy.14
  2.4 0.3 copy.15
  2.8 0.1 copy.13
  2.9 1.1 fusion.2.refs_3_
  4.1 0.5 fusion.3
  4.6 0.8 pad_maximum_fusion
  5.5 0.1 copy-done.2
  5.6 0.1 copy.12
  5.7 0.9 reshape.44.refs_2_
  6.6 0.6 broadcast_in_dim.10.refs_9_
  7.2 68.6 %gather.1 = (bf16[8,256,128]{2,1,0:T(8,128)(2,1)}, bf16[8,2,256,128]{3,2,1,0:T(8,128)(2,1)}, bf16[8,2,256,128]{3,2,1,0:T(8,128)(2,1)}, s32[8,8,128]{2,1,0:T(8,12...) custom-call(bf16[128,4096]{1,0:T(8,128)(2,1)} %bitcast.25, bf16[1,4096]{1,0:T(2,128)(2,1)} %refs_1_.1, ...), custom_call_target="tpu_custom_call" | custom-call | tf_op jit(solution)/shard_map/gather/pallas_call | solution.py:830
  75.8 5.8 %attend.1 = (bf16[256,1024]{1,0:T(8,128)(2,1)}, f32[16,256]{1,0:T(8,128)}) custom-call(bf16[8,256,128]{2,1,0:T(8,128)(2,1)} %get-tuple-element.16.q_ref, bf16[8,512,128]{2,1,0:T(8,128)(2,1)} %bitcast.27, bf16[8,512,128]{2,1,0:T(8,128)(2,1)} %bitcast.28, s32[8,8,128]{2,1,0:T(8,128)} %get-tuple-element.19.doc_ref.doc_smem, ...), custom_call_target="tpu_custom_call" | custom-call | tf_op jit(solution)/shard_map/attend/pallas_call | solution.py:882
  81.6 62.1 %adapt.1 = (bf16[128,2048]{1,0:T(8,128)(2,1)}, bf16[128,4096]{1,0:T(8,128)(2,1)}, f32[16,2048]{1,0:T(8,128)}, f32[16,4096]{1,0:T(8,128)}) custom-call(bf16[256,1024]{1,0:T(8,128)(2,1)} %get-tuple-element.21.refs_0_, f32[16,256]{1,0:T(8,128)} %get-tuple-element.22.refs_1_, bf16[128,4096]{1,0:T(8,128)(2,1)} %bitcast.21, bf16[16,4096]{1,0:T(8,128)(2,1)} %bitcast.31, ...), custom_call_target="tpu_custom_call" | custom-call | tf_op jit(solution)/shard_map/adapt/pallas_call | solution.py:909
  143.7 2.0 %copy.20 = bf16[1,128,2048]{2,1,0:T(8,128)(2,1)} copy(bf16[1,128,2048]{2,1,0:T(8,128)(2,1)} %bitcast.29) | data formatting | bytes 1048576
  145.6 1.0 copy.21
  146.6 0.1 copy-done.4
  146.7 0.7 copy.22
  147.3 0.3 copy-done.3
  147.7 0.7 copy.23
  (11 shorter events, 0.0 us)
Async XLA Ops:
  0.6 1.0 copy-start
  4.6 1.0 copy-start.2
  5.7 0.9 copy-start.5
  143.7 2.0 %copy-start.1 = (bf16[128,4096]{1,0:T(8,128)(2,1)S(1)}, bf16[128,4096]{1,0:T(8,128)(2,1)}, u32[]{:S(2)}) copy-start(bf16[128,4096]{1,0:T(8,128)(2,1)} %get-tuple-element.25) | copy-start | bytes 3145732
  145.6 1.0 copy-start.4
  146.7 1.0 copy-start.3

commit v2 on v1

v2 whole, which is shorter than its diff:
```python
import math

import jax
import jax.numpy as jnp
from jax import lax
from jax.experimental import pallas as pl
from jax.experimental.pallas import tpu as pltpu
from jax.sharding import PartitionSpec as P

MESH = pl.DeviceIdType.MESH
NY = 4
F32 = jnp.float32
BF16 = jnp.bfloat16


def remote(src, dst, send_sem, recv_sem, **where):
    return pltpu.make_async_remote_copy(
        src_ref=src,
        dst_ref=dst,
        send_sem=send_sem,
        recv_sem=recv_sem,
        device_id=where,
        device_id_type=MESH,
    )


def position():
    ctx = lax.axis_index("ctx")
    return ctx // NY, ctx % NY, lax.axis_index("tp")


class Ring:
    def __init__(self, nz, block, half, send, recv, sib_send=None, sib_recv=None):
        self.nz, self.steps = nz, nz // 2
        self.block, self.half = block, half
        self.send, self.recv = send, recv
        self.sib_send, self.sib_recv = sib_send, sib_recv
        self.z, self.y, self.t = position()

    def origin(self, d, s):
        return (self.z - s + self.nz) % self.nz if d == 0 else (self.z + s) % self.nz

    def neighbour(self, d):
        z = (self.z + 1) % self.nz if d == 0 else (self.z + self.nz - 1) % self.nz
        return dict(ctx=z * NY + self.y, tp=self.t)

    def piece(self, zi, d, s):
        return self.half(zi, d, self.t) if s == self.steps else self.block(zi, self.t)

    def hop(self, d, s, src=None):
        piece = self.piece(self.origin(d, s - 1), d, s)
        return remote(
            piece if src is None else src,
            piece,
            self.send.at[d, s - 1],
            self.recv.at[d, s - 1],
            **self.neighbour(d),
        )

    def arrival(self, d, s):
        piece = self.piece(self.origin(d, s), d, s)
        return remote(
            piece, piece, self.send.at[d, s - 1], self.recv.at[d, s - 1], **self.neighbour(d)
        )

    def aside(self, index, zi, core, src=None):
        piece = self.block(zi, core)
        return remote(
            piece if src is None else src,
            piece,
            self.sib_send.at[index],
            self.sib_recv.at[index],
            tp=1 - self.t,
        )

    def start(self, src=None):
        for d in (0, 1):
            self.hop(d, 1, src).start()
        if self.sib_send is not None:
            self.aside(0, self.z, self.t, src).start()

    def step(self, s):
        for d in (0, 1):
            self.arrival(d, s).wait_recv()
            self.hop(d, s + 1).start()
            if self.sib_send is not None:
                self.aside(2 * s - 1 + d, self.origin(d, s), self.t).start()

    def final(self):
        for d in (0, 1):
            self.arrival(d, self.steps).wait_recv()
        if self.sib_send is not None:
            self.aside(self.nz - 1, self.origin(0, self.steps), self.t).start()

    def asides(self):
        yield 0, self.z
        for s in range(1, self.steps):
            for d in (0, 1):
                yield 2 * s - 1 + d, self.origin(d, s)
        yield self.nz - 1, self.origin(0, self.steps)

    def wait_aside(self, index, zi):
        self.aside(index, zi, 1 - self.t).wait_recv()

    def wait_sibling(self):
        for index, zi in self.asides():
            self.wait_aside(index, zi)

    def drain(self):
        for d in (0, 1):
            for s in range(1, self.steps + 1):
                self.hop(d, s).wait_send()
        if self.sib_send is not None:
            for index, zi in self.asides():
                self.aside(index, zi, self.t).wait_send()


def main_kernel(
    nz,
    sections,
    hid_ref,
    gain_ref,
    w_ref,
    q_ref,
    cos_ref,
    sin_ref,
    grad_ref,
    up_ref,
    down_ref,
    doc_ref,
    att_out,
    low_out,
    all_buf,
    sq_all,
    w_buf,
    normed,
    x_buf,
    square_src,
    square_in,
    back_part,
    back_in,
    back_own,
    back_all,
    down_buf,
    doc_in,
    doc_all,
    k_part,
    k_in,
    v_part,
    v_in,
    k_all,
    v_all,
    q_all,
    bias_ref,
    top,
    total,
    acc,
    att,
    low_src,
    low_in,
    red_src,
    red_in,
    dred_src,
    dred_in,
    sq_src,
    sq_in,
    w_send,
    w_recv,
    ws_send,
    ws_recv,
    kv_send,
    kv_recv,
    kvs_send,
    kvs_recv,
    d_send,
    d_recv,
    x_send,
    x_recv,
    q_send,
    q_recv,
    rs_send,
    rs_recv,
    dy_send,
    dy_recv,
    pair_send,
    pair_recv,
    back_send,
    back_recv,
    att_send,
    att_recv,
    low_send,
    low_recv,
    red_send,
    red_recv,
    dred_send,
    dred_recv,
    all_send,
    all_recv,
    sq_send,
    sq_recv,
    sqa_send,
    sqa_recv,
):
    z, y, t = position()
    section = lax.axis_index("section")
    rows, width = hid_ref.shape
    depth = w_ref.shape[1]
    cols = depth * nz // 2
    head_dim = k_all.shape[-1]
    heads = q_all.shape[0]
    toks = 2 * rows
    keys = 2 * toks
    rank = up_ref.shape[0]
    count = nz * NY
    me = z * NY + y
    steps = nz // 2
    home = y // 2
    sibling = dict(tp=1 - t)
    peers = [(osec, ot) for osec in range(sections) for ot in range(2) if osec or ot]

    barrier = pltpu.get_barrier_semaphore()

    def greet(**where):
        pl.semaphore_signal(barrier, inc=1, device_id=where, device_id_type=MESH)

    greet(ctx=(z + 1) % nz * NY + y)
    greet(ctx=(z + nz - 1) % nz * NY + y)
    for oy in range(NY):
        for ot in range(2):
            if oy or ot:
                greet(ctx=z * NY + (y + oy) % NY, tp=(t + ot) % 2)
    for osec, ot in peers:
        if osec:
            greet(section=(section + osec) % sections, tp=(t + ot) % 2)
    pl.semaphore_wait(barrier, 2 + 2 * NY - 1 + 2 * (sections - 1))

    def w_block(p):
        return lambda zi, core: w_buf.at[p, core, pl.ds(pl.multiple_of(zi * depth, depth), depth)]

    def w_half(p):
        return lambda zi, h, core: w_buf.at[
            p, core, pl.ds(pl.multiple_of(zi * depth + h * (depth // 2), depth // 2), depth // 2)
        ]

    def kv_block(buf):
        return lambda zi, core: buf.at[zi, core]

    def kv_half(buf):
        size = buf.shape[2] // 2
        return lambda zi, h, core: buf.at[zi, core, pl.ds(h * size, size)]

    w_rings = [
        Ring(nz, w_block(p), w_half(p), w_send.at[p], w_recv.at[p], ws_send.at[p], ws_recv.at[p])
        for p in (0, 1)
    ]
    kv_rings = [
        Ring(nz, kv_block(buf), kv_half(buf), kv_send.at[p], kv_recv.at[p], kvs_send.at[p], kvs_recv.at[p])
        for p, buf in ((0, k_all), (1, v_all))
    ]

    w_rings[0].start(w_ref.at[0])
    w_rings[1].start(w_ref.at[1])

    doc_own = doc_in.at[0]
    doc_in[0] = jnp.broadcast_to(doc_ref[...], doc_in.shape[1:])

    def doc_copy(oy):
        return remote(
            doc_own,
            doc_in.at[oy],
            dy_send.at[oy - 1],
            dy_recv.at[oy - 1],
            ctx=z * NY + (y + oy) % NY,
        )

    for oy in range(1, NY):
        doc_copy(oy).start()

    def down_copy(core):
        return remote(down_ref, down_buf.at[core], pair_send.at[0], pair_recv.at[0], **sibling)

    hid = hid_ref[...].astype(F32)
    square = jnp.sum(hid * hid, axis=1, keepdims=True)
    square_src[...] = jnp.broadcast_to(square, square_src.shape)
    square_copy = remote(square_src, square_in, pair_send.at[1], pair_recv.at[1], **sibling)
    square_copy.start()
    down_copy(t).start()
    down_buf[t] = down_ref[...]
    own_rows = pl.ds(pl.multiple_of(z * depth, depth), depth)
    w_buf[0, t, own_rows, :] = w_ref[0]
    w_buf[1, t, own_rows, :] = w_ref[1]
    square_copy.wait_recv()
    mean = (square_src[:, :1] + square_in[:, :1]) * (1.0 / (2 * width))
    scale = lax.rsqrt(mean + 1e-06)

    def x_dest(b, core):
        return x_buf.at[pl.ds(b * rows, rows), pl.ds(pl.multiple_of(core * cols, cols), cols)]

    def x_copy(oy):
        yd = (y + oy) % NY
        return remote(
            normed.at[yd],
            x_dest(y % 2, t),
            x_send.at[oy],
            x_recv.at[y % 2, t],
            ctx=z * NY + yd,
            tp=home,
        )

    for yd in range(NY):
        for zl in range(nz // 2):
            start = (zl * NY + yd) * depth
            piece = hid_ref[:, start : start + depth].astype(F32)
            gain = gain_ref[:, start : start + depth].astype(F32)
            normed[yd, :, zl * depth : (zl + 1) * depth] = (piece * scale * gain).astype(BF16)
    for oy in range(1, NY):
        x_copy(oy).start()

    @pl.when(t != home)
    def _():
        x_copy(0).start()

    @pl.when(t == home)
    def _():
        x_buf[
            pl.ds(pl.multiple_of((y % 2) * rows, rows), rows),
            pl.ds(pl.multiple_of(t * cols, cols), cols),
        ] = normed[y]

    def q_dest(b):
        return q_all.at[:, pl.ds(b * rows, rows)]

    def q_copy(kvl):
        return remote(
            q_ref.at[kvl],
            q_dest(y % 2),
            q_send.at[kvl],
            q_recv.at[y % 2],
            ctx=z * NY + 2 * t + kvl,
            tp=home,
        )

    def home_own(kvl):
        return jnp.logical_and(2 * t + kvl == y, home == t)

    for kvl in range(2):

        @pl.when(jnp.logical_not(home_own(kvl)))
        def _():
            q_copy(kvl).start()

        @pl.when(home_own(kvl))
        def _():
            q_all[:, pl.ds(pl.multiple_of((y % 2) * rows, rows), rows), :] = q_ref[kvl]

    for oy in range(1, NY):
        doc_copy(oy).wait_recv()
    line = lax.broadcasted_iota(jnp.int32, doc_in.shape[1:], 0)
    group = jnp.where(line == y, doc_in[0], 0)
    for oy in range(1, NY):
        group = jnp.where(line == (y + NY - oy) % NY, doc_in[oy], group)
    doc_all[z] = group

    def doc_pass(d, s):
        zi = (z - s + 1 + nz) % nz if d == 0 else (z + s - 1) % nz
        to = (z + 1) % nz if d == 0 else (z + nz - 1) % nz
        return remote(
            doc_all.at[zi], doc_all.at[zi], d_send.at[d, s - 1], d_recv.at[d, s - 1], ctx=to * NY + y
        )

    def doc_arrive(d, s):
        zi = (z - s + nz) % nz if d == 0 else (z + s) % nz
        to = (z + 1) % nz if d == 0 else (z + nz - 1) % nz
        return remote(
            doc_all.at[zi], doc_all.at[zi], d_send.at[d, s - 1], d_recv.at[d, s - 1], ctx=to * NY + y
        )

    doc_hops = [(0, s) for s in range(1, steps + 1)] + [(1, s) for s in range(1, steps)]

    def doc_step(s):
        for d in (0, 1):
            if (d, s) in doc_hops:
                doc_arrive(d, s).wait_recv()
                if (d, s + 1) in doc_hops:
                    doc_pass(d, s + 1).start()

    for d in (0, 1):
        if (d, 1) in doc_hops:
            doc_pass(d, 1).start()

    back_part[...] = lax.dot_general(
        up_ref[...], grad_ref[...], (((1,), (1,)), ((), ())), preferred_element_type=F32
    )
    back_copy = remote(back_part, back_in, pair_send.at[2], pair_recv.at[2], **sibling)
    back_copy.start()

    def back_pass(oy):
        return remote(
            back_own,
            back_all.at[y % 2],
            back_send.at[oy - 1],
            back_recv.at[y % 2],
            ctx=z * NY + (y + oy) % NY,
        )

    for s in range(1, steps):
        w_rings[0].step(s)
        w_rings[1].step(s)
        doc_step(s)
        if s == 1:
            back_copy.wait_recv()
            back_own[...] = (back_part[...] + back_in[...]).astype(BF16)

            @pl.when(t == home)
            def _():
                for oy in range(1, NY):
                    back_pass(oy).start()
                back_all[y % 2] = back_own[...]

    def x_wait():
        for b in range(2):
            for core in range(2):

                @pl.when(jnp.logical_or(2 * t + b != y, t != core))
                def _():
                    dest = x_dest(b, core)
                    remote(dest, dest, x_send.at[0], x_recv.at[b, core], **sibling).wait_recv()

    def project(p, part):
        for core in range(2):
            partial = jnp.dot(x_buf[...], w_buf[p, core], preferred_element_type=F32)
            for hl in range(2):
                part[2 * core + hl] = partial[:, hl * head_dim : (hl + 1) * head_dim].astype(part.dtype)

    def scatter_copy(p, oy):
        part, into = ((k_part, k_in), (v_part, v_in))[p]
        yd = (y + oy) % NY
        return remote(
            part.at[yd],
            into.at[oy - 1],
            rs_send.at[p, oy - 1],
            rs_recv.at[p, oy - 1],
            ctx=z * NY + yd,
        )

    def collect(p):
        part, into = ((k_part, k_in), (v_part, v_in))[p]
        for oy in range(1, NY):
            scatter_copy(p, oy).wait_recv()
        whole = part[y].astype(F32)
        for oy in range(1, NY):
            whole = whole + into[oy - 1].astype(F32)
        return whole

    def rope(v):
        return (v * cos_ref[...] + pltpu.roll(v, head_dim // 2, 1) * sin_ref[...]).astype(BF16)

    x_wait()
    w_rings[0].final()
    w_rings[0].wait_sibling()
    project(0, k_part)
    for oy in range(1, NY):
        scatter_copy(0, oy).start()
    w_rings[1].final()
    w_rings[1].wait_sibling()
    project(1, v_part)
    for oy in range(1, NY):
        scatter_copy(1, oy).start()

    for b in range(2):

        @pl.when(jnp.logical_or(2 * t + b != y, home != t))
        def _():
            dest = q_dest(b)
            remote(dest, dest, q_send.at[0], q_recv.at[b], **sibling).wait_recv()

    for h in range(heads):
        q_all[h] = rope(q_all[h].astype(F32))
    doc_step(steps)
    q_doc = jnp.concatenate(
        [
            jnp.sum(jnp.where(line == 2 * t + b, doc_all[z].astype(F32), 0.0), axis=0, keepdims=True)
            for b in range(2)
        ],
        axis=1,
    )

    k_all[z, t] = rope(collect(0))
    kv_rings[0].start()
    v_all[z, t] = jnp.transpose(collect(1)).astype(BF16)
    kv_rings[1].start()

    factor = head_dim ** (-0.5) * math.log2(math.e)

    def block(kb, first):
        turned = jnp.transpose(doc_all[kb].astype(F32))
        k_doc = jnp.concatenate([turned[:, j : j + 1] for j in range(NY)], axis=0)
        allowed = k_doc == q_doc
        if first:
            q_pos = t * toks + lax.broadcasted_iota(jnp.int32, (keys, toks), 1)
            k_pos = lax.broadcasted_iota(jnp.int32, (keys, toks), 0)
            allowed = jnp.logical_and(allowed, k_pos <= q_pos)
        bias_ref[...] = jnp.where(allowed, 0.0, -1e30)

        def head(h):
            q = q_all[h]
            scores = [
                lax.dot_general(
                    k_all[kb, core], q, (((1,), (1,)), ((), ())), preferred_element_type=F32
                )
                + bias_ref[core * toks : (core + 1) * toks, :]
                for core in range(2)
            ]
            peak = jnp.maximum(
                jnp.max(scores[0], axis=0, keepdims=True), jnp.max(scores[1], axis=0, keepdims=True)
            )
            if first:
                new_top = peak
            else:
                old_top = top[h]
                new_top = jnp.maximum(old_top, peak)
                shrink = jnp.exp2((old_top - new_top) * factor)
            weights = [jnp.exp2((s - new_top) * factor) for s in scores]
            part_sum = jnp.sum(weights[0], axis=0, keepdims=True) + jnp.sum(
                weights[1], axis=0, keepdims=True
            )
            part = jnp.dot(
                v_all[kb, 0], weights[0].astype(BF16), preferred_element_type=F32
            ) + jnp.dot(v_all[kb, 1], weights[1].astype(BF16), preferred_element_type=F32)
            top[h] = new_top
            if first:
                total[h] = part_sum
                acc[h] = part
            else:
                total[h] = total[h] * shrink + part_sum
                acc[h] = acc[h] * shrink + part

        def pair(i, carry):
            head(2 * i)
            head(2 * i + 1)
            return carry

        lax.fori_loop(0, heads // 2, pair, 0)

    def await_aside(index, zi):
        for ring in kv_rings:
            ring.wait_aside(index, zi)

    def attend_step(s):
        for d in (0, 1):
            zi = kv_rings[0].origin(d, s)
            await_aside(2 * s - 1 + d, zi)

            @pl.when(zi < z)
            def _():
                block(zi, False)

    await_aside(0, z)
    block(z, True)
    for s in range(1, steps):
        kv_rings[0].step(s)
        kv_rings[1].step(s)
        if s > 1:
            attend_step(s - 1)
    if steps > 1:
        attend_step(steps - 1)
    kv_rings[0].final()
    kv_rings[1].final()
    last = kv_rings[0].origin(0, steps)
    await_aside(nz - 1, last)

    @pl.when(last < z)
    def _():
        block(last, False)

    down_copy(1 - t).wait_recv()
    half_cols = heads * head_dim
    low = None
    for h in range(heads):
        out = acc[h] / total[h]
        factor_cols = down_buf[
            home, :, pl.ds(pl.multiple_of((y % 2) * half_cols + h * head_dim, head_dim), head_dim)
        ]
        part = jnp.dot(factor_cols, out.astype(BF16), preferred_element_type=F32)
        low = part if low is None else low + part
        att[:, h * head_dim : (h + 1) * head_dim] = jnp.transpose(out).astype(BF16)

    def low_copy(b, core):
        return remote(
            low_src.at[b],
            low_in.at[y],
            low_send.at[b, core],
            low_recv.at[y],
            ctx=z * NY + 2 * t + b,
            tp=core,
        )

    def low_own(b, core):
        return jnp.logical_and(2 * t + b == y, t == core)

    for b in range(2):
        low_src[b] = low[:, b * rows : (b + 1) * rows]
    for b in range(2):
        for core in range(2):

            @pl.when(jnp.logical_not(low_own(b, core)))
            def _():
                low_copy(b, core).start()

            @pl.when(low_own(b, core))
            def _():
                low_in[y] = low_src[b]

    for b in range(2):

        @pl.when(2 * t + b != y)
        def _():
            remote(
                back_all.at[b], back_all.at[b], back_send.at[0], back_recv.at[b], **sibling
            ).wait_recv()

    back = jnp.concatenate([back_all[0], back_all[1]], axis=1)
    down_part = jnp.dot(back, att[...], preferred_element_type=F32)
    for r in range(2):
        for h in range(heads):
            dred_src[r * heads + h] = down_part[8 * r : 8 * r + 8, h * 128 : (h + 1) * 128].astype(BF16)
    blocks = count // 2

    def dred_owner(i):
        return (i // heads) * blocks + (y % 2) * heads + i % heads

    def dred_copy(i):
        return remote(
            dred_src.at[i],
            dred_in.at[2 * z + t],
            dred_send.at[i],
            dred_recv.at[2 * z + t],
            ctx=dred_owner(i),
            tp=home,
        )

    def dred_own(i):
        return jnp.logical_and(dred_owner(i) == me, home == t)

    def dred_start(i, carry):
        @pl.when(jnp.logical_not(dred_own(i)))
        def _():
            dred_copy(i).start()

        @pl.when(dred_own(i))
        def _():
            dred_in[2 * z + t] = dred_src[i]

        return carry

    lax.fori_loop(0, 2 * heads, dred_start, 0)

    for src_y in range(NY):

        @pl.when(jnp.logical_or(src_y != y, home != t))
        def _():
            remote(
                low_in.at[src_y], low_in.at[src_y], low_send.at[0, 0], low_recv.at[src_y], **sibling
            ).wait_recv()

    low = low_in[0]
    for src_y in range(1, NY):
        low = low + low_in[src_y]
    low = low.astype(BF16)
    low_out[...] = low

    for c in range(count):
        red_src[c] = jnp.dot(
            low, grad_ref[:, c * 128 : (c + 1) * 128], preferred_element_type=F32
        ).astype(BF16)

    def red_copy(o):
        to = (me + o) % count
        return remote(
            red_src.at[to], red_in.at[o - 1], red_send.at[o - 1], red_recv.at[o - 1], ctx=to
        )

    def red_start(o, carry):
        red_copy(o).start()
        return carry

    lax.fori_loop(1, count, red_start, 0)

    def att_dest(kvl):
        return att_out.at[:, pl.ds(pl.multiple_of(kvl * half_cols, half_cols), half_cols)]

    def att_copy(b):
        return remote(
            att.at[pl.ds(b * rows, rows)],
            att_dest(y % 2),
            att_send.at[b],
            att_recv.at[y % 2],
            ctx=z * NY + 2 * t + b,
            tp=home,
        )

    for b in range(2):

        @pl.when(jnp.logical_not(home_own(b)))
        def _():
            att_copy(b).start()

        @pl.when(home_own(b))
        def _():
            att_out[:, pl.ds(pl.multiple_of((y % 2) * half_cols, half_cols), half_cols)] = att[
                b * rows : (b + 1) * rows
            ]

    down_y = 2 * t + (me % blocks) // heads

    def dred_add(i, carry):
        @pl.when(jnp.logical_or(down_y != y, i != 2 * z + t))
        def _():
            remote(
                dred_in.at[i], dred_in.at[i], dred_send.at[0], dred_recv.at[i], **sibling
            ).wait_recv()

        return carry + dred_in[i].astype(F32)

    down_sum = lax.fori_loop(0, 2 * nz, dred_add, jnp.zeros((8, 128), F32))

    def red_add(o, so_far):
        red_copy(o).wait_recv()
        return so_far + red_in[o - 1].astype(F32)

    up_sum = lax.fori_loop(1, count, red_add, red_src[me].astype(F32))
    all_buf[me] = jnp.concatenate([up_sum, down_sum], axis=0).astype(BF16)
    squares = jnp.sum(up_sum * up_sum, axis=0, keepdims=True) + jnp.sum(
        down_sum * down_sum, axis=0, keepdims=True
    )
    sq_src[...] = jnp.broadcast_to(jnp.sum(squares, axis=1, keepdims=True), sq_src.shape)

    def sq_copy(i):
        osec, ot = peers[i]
        return remote(
            sq_src,
            sq_in.at[i],
            sq_send.at[i],
            sq_recv.at[i],
            section=(section + osec) % sections,
            tp=(t + ot) % 2,
        )

    for i in range(len(peers)):
        sq_copy(i).start()

    def spread(buf, sends, recvs):
        def copy(o):
            to = (me + o) % count
            return remote(buf.at[me], buf.at[me], sends.at[o - 1], recvs.at[o - 1], ctx=to)

        def arrive(o):
            of = (me - o + count) % count
            return remote(buf.at[of], buf.at[of], sends.at[o - 1], recvs.at[o - 1], ctx=of)

        def each(act):
            def one(o, carry):
                act(o)
                return carry

            lax.fori_loop(1, count, one, 0)

        return (
            lambda: each(lambda o: copy(o).start()),
            lambda: each(lambda o: arrive(o).wait_recv()),
            lambda: each(lambda o: copy(o).wait_send()),
        )

    all_start, all_wait, all_drain = spread(all_buf, all_send, all_recv)
    sqa_start, sqa_wait, sqa_drain = spread(sq_all, sqa_send, sqa_recv)
    all_start()
    squares = sq_src[...]
    for i in range(len(peers)):
        sq_copy(i).wait_recv()
        squares = squares + sq_in[i]
    sq_all[me] = squares
    sqa_start()

    for ring in w_rings + kv_rings:
        ring.drain()
    for oy in range(1, NY):
        doc_copy(oy).wait_send()
        x_copy(oy).wait_send()
        scatter_copy(0, oy).wait_send()
        scatter_copy(1, oy).wait_send()

    @pl.when(t != home)
    def _():
        x_copy(0).wait_send()

    @pl.when(t == home)
    def _():
        for oy in range(1, NY):
            back_pass(oy).wait_send()

    for d, s in doc_hops:
        doc_pass(d, s).wait_send()
    down_copy(t).wait_send()
    square_copy.wait_send()
    back_copy.wait_send()
    for b in range(2):

        @pl.when(jnp.logical_not(home_own(b)))
        def _():
            q_copy(b).wait_send()
            att_copy(b).wait_send()

        for core in range(2):

            @pl.when(jnp.logical_not(low_own(b, core)))
            def _():
                low_copy(b, core).wait_send()

    def dred_drain(i, carry):
        @pl.when(jnp.logical_not(dred_own(i)))
        def _():
            dred_copy(i).wait_send()

        return carry

    lax.fori_loop(0, 2 * heads, dred_drain, 0)

    def red_drain(o, carry):
        red_copy(o).wait_send()
        return carry

    lax.fori_loop(1, count, red_drain, 0)
    for kvl in range(2):

        @pl.when(jnp.logical_or(2 * t + kvl != y, home != t))
        def _():
            dest = att_dest(kvl)
            remote(dest, dest, att_send.at[0], att_recv.at[kvl], **sibling).wait_recv()

    all_wait()
    all_drain()
    for i in range(len(peers)):
        sq_copy(i).wait_send()
    sqa_wait()
    sqa_drain()


def finish_kernel(ceiling, att_ref, low_ref, all_ref, sq_ref, up_ref, att_out, adapter_out, gdown_out, gup_out):
    count = all_ref.shape[0]
    rank = low_ref.shape[0]
    blocks = count // 2
    norm = sq_ref[0]
    for c in range(1, count):
        norm = norm + sq_ref[c]
    clip = jnp.minimum(1.0, ceiling / (jnp.sqrt(norm[0:1, 0:1]) + 1e-06))
    for c in range(count):
        r0 = 8 * (c // blocks)
        c0 = 128 * (c % blocks)
        gup_out[:, c * 128 : (c + 1) * 128] = all_ref[c, 0:rank, :].astype(F32) * clip
        gdown_out[r0 : r0 + 8, c0 : c0 + 128] = all_ref[c, rank : rank + 8, :].astype(F32) * clip
    att_out[...] = att_ref[...]
    adapter_out[...] = lax.dot_general(
        low_ref[...], up_ref[...], (((0,), (0,)), ((), ())), preferred_element_type=F32
    ).astype(BF16)


def rope_tables(positions, head_dim):
    lane = jnp.arange(head_dim, dtype=jnp.int32)
    half = head_dim // 2
    freqs = 1000000.0 ** (-(lane % half).astype(F32) * 2.0 / head_dim)
    angles = positions.astype(F32)[:, None] * freqs[None, :]
    return jnp.cos(angles), jnp.where(lane[None, :] < half, -jnp.sin(angles), jnp.sin(angles))


def per_device(hidden, gain, queries, key_value_weight, adapt_down, adapt_up, out_grad, doc_ids):
    nz = lax.axis_size("ctx") // NY
    sections = lax.axis_size("section")
    rows, width = hidden.shape[1:]
    depth, kv_count = key_value_weight.shape[1:3]
    head_dim = key_value_weight.shape[-1]
    heads = queries.shape[2]
    group = heads // kv_count
    rank, local_query = adapt_down.shape[1:]
    toks = 2 * rows
    z, y, t = position()

    start = (z * 2 + t) * toks
    cos, sin = rope_tables(start + jnp.arange(toks, dtype=jnp.int32), head_dim)
    q = queries[0].transpose(1, 0, 2).reshape(kv_count, group, rows, head_dim)
    w = key_value_weight[0].transpose(2, 0, 1, 3).reshape(2, depth, kv_count * head_dim)

    vmem = pl.BlockSpec(memory_space=pltpu.VMEM)
    dma = pltpu.SemaphoreType.DMA
    steps = nz // 2
    count = nz * NY
    peers = 2 * sections - 1
    chunk = rank + 8
    att, low, summed, squares = pl.pallas_call(
        lambda *refs: main_kernel(nz, sections, *refs),
        out_shape=(
            jax.ShapeDtypeStruct((rows, local_query), BF16),
            jax.ShapeDtypeStruct((rank, rows), BF16),
            jax.ShapeDtypeStruct((count, chunk, 128), BF16),
            jax.ShapeDtypeStruct((count, 8, 128), F32),
        ),
        in_specs=[vmem] * 10,
        out_specs=[vmem] * 4,
        scratch_shapes=[
            pltpu.VMEM((2, 2, nz * depth, kv_count * head_dim), BF16),
            pltpu.VMEM((NY, rows, depth * nz // 2), BF16),
            pltpu.VMEM((toks, depth * nz), BF16),
            pltpu.VMEM((rows, 128), F32),
            pltpu.VMEM((rows, 128), F32),
            pltpu.VMEM((rank, rows), F32),
            pltpu.VMEM((rank, rows), F32),
            pltpu.VMEM((rank, rows), BF16),
            pltpu.VMEM((2, rank, rows), BF16),
            pltpu.VMEM((2, rank, local_query), BF16),
            pltpu.VMEM((NY, 8, rows), jnp.int32),
            pltpu.VMEM((nz, 8, rows), jnp.int32),
            pltpu.VMEM((NY, toks, head_dim), F32),
            pltpu.VMEM((NY - 1, toks, head_dim), F32),
            pltpu.VMEM((NY, toks, head_dim), BF16),
            pltpu.VMEM((NY - 1, toks, head_dim), BF16),
            pltpu.VMEM((nz, 2, toks, head_dim), BF16),
            pltpu.VMEM((nz, 2, head_dim, toks), BF16),
            pltpu.VMEM((group, toks, head_dim), BF16),
            pltpu.VMEM((2 * toks, toks), F32),
            pltpu.VMEM((group, 1, toks), F32),
            pltpu.VMEM((group, 1, toks), F32),
            pltpu.VMEM((group, head_dim, toks), F32),
            pltpu.VMEM((toks, group * head_dim), BF16),
            pltpu.VMEM((2, rank, rows), F32),
            pltpu.VMEM((NY, rank, rows), F32),
            pltpu.VMEM((count, rank, 128), BF16),
            pltpu.VMEM((count - 1, rank, 128), BF16),
            pltpu.VMEM((2 * group, 8, 128), BF16),
            pltpu.VMEM((2 * nz, 8, 128), BF16),
            pltpu.VMEM((8, 128), F32),
            pltpu.VMEM((peers, 8, 128), F32),
            dma((2, 2, steps)),
            dma((2, 2, steps)),
            dma((2, nz)),
            dma((2, nz)),
            dma((2, 2, steps)),
            dma((2, 2, steps)),
            dma((2, nz)),
            dma((2, nz)),
            dma((2, steps)),
            dma((2, steps)),
            dma((NY,)),
            dma((2, 2)),
            dma((2,)),
            dma((2,)),
            dma((2, NY - 1)),
            dma((2, NY - 1)),
            dma((NY - 1,)),
            dma((NY - 1,)),
            dma((3,)),
            dma((3,)),
            dma((NY - 1,)),
            dma((2,)),
            dma((2,)),
            dma((2,)),
            dma((2, 2)),
            dma((NY,)),
            dma((count - 1,)),
            dma((count - 1,)),
            dma((2 * group,)),
            dma((2 * nz,)),
            dma((count - 1,)),
            dma((count - 1,)),
            dma((peers,)),
            dma((peers,)),
            dma((count - 1,)),
            dma((count - 1,)),
        ],
        compiler_params=pltpu.CompilerParams(collective_id=0, has_side_effects=True),
        name="main",
    )(hidden[0], gain, w, q, cos, sin, out_grad[0], adapt_up[0], adapt_down[0], doc_ids[None])

    ceiling = 0.5 * math.sqrt(sections * rank * (local_query + width) * 2)
    return pl.pallas_call(
        lambda *refs: finish_kernel(ceiling, *refs),
        out_shape=(
            jax.ShapeDtypeStruct((rows, local_query), BF16),
            jax.ShapeDtypeStruct((rows, width), BF16),
            jax.ShapeDtypeStruct((rank, local_query), F32),
            jax.ShapeDtypeStruct((rank, width), F32),
        ),
        in_specs=[vmem] * 5,
        out_specs=[vmem] * 4,
        name="finish",
    )(att, low, summed, squares, adapt_up[0])


def solution(mesh):
    def step(*args):
        return tuple(out[None] for out in per_device(*args))

    return jax.shard_map(
        step,
        mesh=mesh,
        in_specs=(
            P("section", "ctx", "tp"),
            P("section", "tp"),
            P("section", "ctx", "tp", None),
            P("section", "ctx", "tp", None, None),
            P("section", None, "tp"),
            P("section", None, "tp"),
            P("section", "ctx", "tp"),
            P("ctx"),
        ),
        out_specs=(
            P("section", "ctx", "tp"),
            P("section", "ctx", "tp"),
            P("section", None, "tp"),
            P("section", None, "tp"),
        ),
        check_vma=False,
    )
```

time: 149 us -> 116 us (0.78)
  Pallas kernels: 136 us -> 112 us
  local copies, waits for them, and re-layouts: 8.1 us -> 1.97 us
  other arithmetic: 3.03 us -> 1.27 us
    pallas_call x3 -> x2, Pallas kernels: 136 us -> 112 us  [the longest x1 109 us: per_device(): pl.pallas_call(lambda *refs: main_kernel(nz, sections, *refs), out_shape=...]
    unnamed x16 -> x4, local copies, waits for them, and re-layouts: 5.36 us -> 0.03 us
where the time goes in v2:
time: 116 us
  Pallas kernels  112 us (97%)
  local copies, waits for them, and re-layouts  1.97 us (2%)
  other arithmetic  1.27 us (1%)
    pallas_call x1, Pallas kernels, per_device(): pl.pallas_call(lambda *refs: main_kernel(nz, sections, *refs), out_shape=...  109 us
    pallas_call x1, Pallas kernels, per_device(): pl.pallas_call(lambda *refs: finish_kernel(ceiling, *refs), out_shape=(ja...  2.88 us

profile of v2, /device:TPU:1, one launch (start us, length us, event | category | flops | bytes accessed | tf_op | source)
XLA Modules:
  0.0 116.0 jit_solution(3124960284808876507)
XLA Ops:
  0.6 0.0 copy-start.1
  0.7 1.2 %negate_select_fusion = (f32[256,128]{1,0:T(8,128)}, f32[256,128]{1,0:T(8,128)}) fusion(f32[128]{0:T(128)S(1)} %fusion.3, f32[256]{0:T(256)S(1)} %add_convert_fusion, pred[128]{0:T(512)(128)(4,1)S(1)} %iota_compare_fusion), kind=kLoop, calls=%fused_computation | loop fusion | flops 98304 | bytes 263808 | tf_op jit(solution)/shard_map/jit(_where)/select_n | solution.py:872
  1.9 0.0 copy-done.1
  1.9 0.0 copy-start
  1.9 0.1 copy.12
  2.1 0.9 reshape.37.refs_2_
  3.0 0.0 copy-done
  3.0 0.9 copy.13
  3.9 109.2 %main.1 = (bf16[128,2048]{1,0:T(8,128)(2,1)}, bf16[16,128]{1,0:T(8,128)(2,1)}, bf16[32,24,128]{2,1,0:T(8,128)(2,1)}, f32[32,8,128]{2,1,0:T(8,128)}) custom-call(bf16[128,4096]{1,0:T(8,128)(2,1)} %bitcast.17, bf16[1,4096]{1,0:T(2,128)(2,1)} %refs_1_.1, bf16[2,256,256]{2,1,0:T(8,128)(2,1)} %reshape.37.refs_2_, bf16[2,8,128,128]{3,2,1,0:T(8,128)(2,1)} %bitcast.16, ...), custom_call_target="tpu_custom_call" | custom-call | tf_op jit(solution)/shard_map/main/pallas_call | solution.py:898
  113.1 2.9 %finish.1 = (bf16[128,2048]{1,0:T(8,128)(2,1)}, bf16[128,4096]{1,0:T(8,128)(2,1)}, f32[16,2048]{1,0:T(8,128)}, f32[16,4096]{1,0:T(8,128)}) custom-call(bf16[128,2048]{1,0:T(8,128)(2,1)} %get-tuple-element.12.refs_0_, bf16[16,128]{1,0:T(8,128)(2,1)} %get-tuple-element.13.refs_1_, bf16[32,24,128]{2,1,0:T(8,128)(2,1)} %get-tuple-element.14.refs_2_, ...), custom_call_target="tpu_custom_call" | custom-call | tf_op jit(solution)/shard_map/finish/pallas_call | solution.py:983
  (3 shorter events, 0.0 us)
Async XLA Ops:
  0.6 1.3 %copy-start.1 = (bf16[1,256,2,2,128]{4,3,2,1,0:T(2,128)(2,1)S(1)}, bf16[1,256,2,2,128]{4,3,2,1,0:T(2,128)(2,1)}, u32[]{:S(2)}) copy-start(bf16[1,256,2,2,128]{4,3,2,1,0:T(2,128)(2,1)} %param.11) | copy-start | bytes 786436
  1.9 1.0 copy-start

commit v3 on v2

--- a/solution.py
+++ b/solution.py
@@ -118,20 +118,27 @@
 def main_kernel(
     nz,
     sections,
-    hid_ref,
+    hid_hbm,
     gain_ref,
     w_ref,
-    q_ref,
-    cos_ref,
-    sin_ref,
-    grad_ref,
-    up_ref,
-    down_ref,
+    q_hbm,
+    freq_ref,
+    grad_hbm,
+    up_hbm,
+    down_hbm,
     doc_ref,
     att_out,
     low_out,
     all_buf,
     sq_all,
+    hid_ref,
+    q_raw,
+    q_ref,
+    grad_ref,
+    up_ref,
+    down_ref,
+    cos_ref,
+    sin_ref,
     w_buf,
     normed,
     x_buf,
@@ -200,6 +207,8 @@
     sq_recv,
     sqa_send,
     sqa_recv,
+    load_sem,
+    own_sem,
 ):
     z, y, t = position()
     section = lax.axis_index("section")
@@ -232,6 +241,21 @@
     for osec, ot in peers:
         if osec:
             greet(section=(section + osec) % sections, tp=(t + ot) % 2)
+    slab = rows // 4
+    hid_loads = [
+        pltpu.make_async_copy(
+            hid_hbm.at[pl.ds(i * slab, slab)], hid_ref.at[pl.ds(i * slab, slab)], load_sem.at[i]
+        )
+        for i in range(4)
+    ]
+    late_loads = [
+        pltpu.make_async_copy(src, dst, load_sem.at[4 + i])
+        for i, (src, dst) in enumerate(
+            ((q_hbm, q_raw), (grad_hbm, grad_ref), (up_hbm, up_ref), (down_hbm, down_ref))
+        )
+    ]
+    for load in hid_loads:
+        load.start()
     pl.semaphore_wait(barrier, 2 + 2 * NY - 1 + 2 * (sections - 1))
 
     def w_block(p):
@@ -260,6 +284,12 @@
 
     w_rings[0].start(w_ref.at[0])
     w_rings[1].start(w_ref.at[1])
+    own_rows = pl.ds(pl.multiple_of(z * depth, depth), depth)
+    own_loads = [
+        pltpu.make_async_copy(w_ref.at[p], w_buf.at[p, t, own_rows], own_sem.at[p]) for p in (0, 1)
+    ]
+    for load in late_loads + own_loads:
+        load.start()
 
     doc_own = doc_in.at[0]
     doc_in[0] = jnp.broadcast_to(doc_ref[...], doc_in.shape[1:])
@@ -279,16 +309,13 @@
     def down_copy(core):
         return remote(down_ref, down_buf.at[core], pair_send.at[0], pair_recv.at[0], **sibling)
 
-    hid = hid_ref[...].astype(F32)
-    square = jnp.sum(hid * hid, axis=1, keepdims=True)
-    square_src[...] = jnp.broadcast_to(square, square_src.shape)
+    for i, load in enumerate(hid_loads):
+        load.wait()
+        hid = hid_ref[i * slab : (i + 1) * slab, :].astype(F32)
+        square = jnp.sum(hid * hid, axis=1, keepdims=True)
+        square_src[i * slab : (i + 1) * slab, :] = jnp.broadcast_to(square, (slab, 128))
     square_copy = remote(square_src, square_in, pair_send.at[1], pair_recv.at[1], **sibling)
     square_copy.start()
-    down_copy(t).start()
-    down_buf[t] = down_ref[...]
-    own_rows = pl.ds(pl.multiple_of(z * depth, depth), depth)
-    w_buf[0, t, own_rows, :] = w_ref[0]
-    w_buf[1, t, own_rows, :] = w_ref[1]
     square_copy.wait_recv()
     mean = (square_src[:, :1] + square_in[:, :1]) * (1.0 / (2 * width))
     scale = lax.rsqrt(mean + 1e-06)
@@ -327,6 +354,10 @@
             pl.ds(pl.multiple_of(t * cols, cols), cols),
         ] = normed[y]
 
+    late_loads[0].wait()
+    turned_q = jnp.transpose(q_raw[...].astype(F32), (1, 0, 2)).astype(BF16)
+    q_ref[...] = turned_q.reshape(q_ref.shape)
+
     def q_dest(b):
         return q_all.at[:, pl.ds(b * rows, rows)]
 
@@ -388,6 +419,11 @@
         if (d, 1) in doc_hops:
             doc_pass(d, 1).start()
 
+    late_loads[3].wait()
+    down_copy(t).start()
+    down_buf[t] = down_ref[...]
+    late_loads[1].wait()
+    late_loads[2].wait()
     back_part[...] = lax.dot_general(
         up_ref[...], grad_ref[...], (((1,), (1,)), ((), ())), preferred_element_type=F32
     )
@@ -407,6 +443,13 @@
         w_rings[0].step(s)
         w_rings[1].step(s)
         doc_step(s)
+        if s == 2:
+            lane = lax.broadcasted_iota(jnp.int32, cos_ref.shape, 1)
+            token = lax.broadcasted_iota(jnp.int32, cos_ref.shape, 0) + (z * 2 + t) * toks
+            angles = token.astype(F32) * freq_ref[...]
+            cos_ref[...] = jnp.cos(angles)
+            sine = jnp.sin(angles)
+            sin_ref[...] = jnp.where(lane < head_dim // 2, -sine, sine)
         if s == 1:
             back_copy.wait_recv()
             back_own[...] = (back_part[...] + back_in[...]).astype(BF16)
@@ -456,6 +499,8 @@
         return (v * cos_ref[...] + pltpu.roll(v, head_dim // 2, 1) * sin_ref[...]).astype(BF16)
 
     x_wait()
+    for load in own_loads:
+        load.wait()
     w_rings[0].final()
     w_rings[0].wait_sibling()
     project(0, k_part)
@@ -535,35 +580,32 @@
                 total[h] = total[h] * shrink + part_sum
                 acc[h] = acc[h] * shrink + part
 
-        def pair(i, carry):
-            head(2 * i)
-            head(2 * i + 1)
-            return carry
-
-        lax.fori_loop(0, heads // 2, pair, 0)
+        for h in range(heads):
+            head(h)
 
     def await_aside(index, zi):
         for ring in kv_rings:
             ring.wait_aside(index, zi)
 
     def attend_step(s):
-        for d in (0, 1):
-            zi = kv_rings[0].origin(d, s)
+        def one(d, carry):
+            zi = jnp.where(d == 0, z - s + nz, z + s) % nz
             await_aside(2 * s - 1 + d, zi)
 
             @pl.when(zi < z)
             def _():
                 block(zi, False)
+
+            return carry
+
+        lax.fori_loop(0, 2, one, 0)
 
     await_aside(0, z)
     block(z, True)
     for s in range(1, steps):
         kv_rings[0].step(s)
         kv_rings[1].step(s)
-        if s > 1:
-            attend_step(s - 1)
-    if steps > 1:
-        attend_step(steps - 1)
+        attend_step(s)
     kv_rings[0].final()
     kv_rings[1].final()
     last = kv_rings[0].origin(0, steps)
@@ -845,10 +887,69 @@
     sqa_drain()
 
 
-def finish_kernel(ceiling, att_ref, low_ref, all_ref, sq_ref, up_ref, att_out, adapter_out, gdown_out, gup_out):
+def finish_kernel(
+    ceiling,
+    att_hbm,
+    low_hbm,
+    all_hbm,
+    sq_hbm,
+    up_hbm,
+    att_out,
+    adapter_out,
+    gdown_out,
+    gup_out,
+    att_ref,
+    low_ref,
+    all_ref,
+    sq_ref,
+    up_ref,
+    adapter,
+    gdown,
+    gup,
+    in_sem,
+    out_sem,
+):
     count = all_ref.shape[0]
-    rank = low_ref.shape[0]
+    rank, rows = low_ref.shape
+    width = up_ref.shape[1]
     blocks = count // 2
+    ins = [
+        pltpu.make_async_copy(src, dst, in_sem.at[i])
+        for i, (src, dst) in enumerate(
+            (
+                (low_hbm, low_ref),
+                (up_hbm, up_ref),
+                (sq_hbm, sq_ref),
+                (all_hbm, all_ref),
+                (att_hbm.at[pl.ds(0, rows // 2)], att_ref.at[pl.ds(0, rows // 2)]),
+                (att_hbm.at[pl.ds(rows // 2, rows // 2)], att_ref.at[pl.ds(rows // 2, rows // 2)]),
+            )
+        )
+    ]
+    outs = []
+
+    def put(src, dst):
+        copy = pltpu.make_async_copy(src, dst, out_sem.at[len(outs)])
+        copy.start()
+        outs.append(copy)
+
+    for copy in ins:
+        copy.start()
+    ins[0].wait()
+    ins[1].wait()
+    part = rows // 4
+    low = jnp.transpose(low_ref[...].astype(F32)).astype(BF16)
+    for i in range(4):
+        adapter[i * part : (i + 1) * part, :] = jnp.dot(
+            low[i * part : (i + 1) * part], up_ref[...], preferred_element_type=F32
+        ).astype(BF16)
+        put(adapter.at[pl.ds(i * part, part)], adapter_out.at[pl.ds(i * part, part)])
+    for i in range(2):
+        ins[4 + i].wait()
+        half = pl.ds(i * (rows // 2), rows // 2)
+        put(att_ref.at[half], att_out.at[half])
+    ins[2].wait()
+    ins[3].wait()
     norm = sq_ref[0]
     for c in range(1, count):
         norm = norm + sq_ref[c]
@@ -856,20 +957,12 @@
     for c in range(count):
         r0 = 8 * (c // blocks)
         c0 = 128 * (c % blocks)
-        gup_out[:, c * 128 : (c + 1) * 128] = all_ref[c, 0:rank, :].astype(F32) * clip
-        gdown_out[r0 : r0 + 8, c0 : c0 + 128] = all_ref[c, rank : rank + 8, :].astype(F32) * clip
-    att_out[...] = att_ref[...]
-    adapter_out[...] = lax.dot_general(
-        low_ref[...], up_ref[...], (((0,), (0,)), ((), ())), preferred_element_type=F32
-    ).astype(BF16)
-
-
-def rope_tables(positions, head_dim):
-    lane = jnp.arange(head_dim, dtype=jnp.int32)
-    half = head_dim // 2
-    freqs = 1000000.0 ** (-(lane % half).astype(F32) * 2.0 / head_dim)
-    angles = positions.astype(F32)[:, None] * freqs[None, :]
-    return jnp.cos(angles), jnp.where(lane[None, :] < half, -jnp.sin(angles), jnp.sin(angles))
+        gup[:, c * 128 : (c + 1) * 128] = all_ref[c, 0:rank, :].astype(F32) * clip
+        gdown[r0 : r0 + 8, c0 : c0 + 128] = all_ref[c, rank : rank + 8, :].astype(F32) * clip
+    put(gup, gup_out)
+    put(gdown, gdown_out)
+    for copy in outs:
+        copy.wait()
 
 
 def per_device(hidden, gain, queries, key_value_weight, adapt_down, adapt_up, out_grad, doc_ids):
@@ -882,14 +975,13 @@
     group = heads // kv_count
     rank, local_query = adapt_down.shape[1:]
     toks = 2 * rows
-    z, y, t = position()
-
-    start = (z * 2 + t) * toks
-    cos, sin = rope_tables(start + jnp.arange(toks, dtype=jnp.int32), head_dim)
-    q = queries[0].transpose(1, 0, 2).reshape(kv_count, group, rows, head_dim)
+    half = head_dim // 2
+    freqs = 1000000.0 ** (-jnp.arange(half, dtype=F32) * 2.0 / head_dim)
+    freqs = jnp.concatenate([freqs, freqs])[None]
     w = key_value_weight[0].transpose(2, 0, 1, 3).reshape(2, depth, kv_count * head_dim)
 
     vmem = pl.BlockSpec(memory_space=pltpu.VMEM)
+    hbm = pl.BlockSpec(memory_space=pl.ANY)
     dma = pltpu.SemaphoreType.DMA
     steps = nz // 2
     count = nz * NY
@@ -903,9 +995,17 @@
             jax.ShapeDtypeStruct((count, chunk, 128), BF16),
             jax.ShapeDtypeStruct((count, 8, 128), F32),
         ),
-        in_specs=[vmem] * 10,
+        in_specs=[hbm, vmem, hbm, hbm, vmem, hbm, hbm, hbm, vmem],
         out_specs=[vmem] * 4,
         scratch_shapes=[
+            pltpu.VMEM((rows, width), BF16),
+            pltpu.VMEM((rows, heads, head_dim), BF16),
+            pltpu.VMEM((kv_count, group, rows, head_dim), BF16),
+            pltpu.VMEM((rows, width), BF16),
+            pltpu.VMEM((rank, width), BF16),
+            pltpu.VMEM((rank, local_query), BF16),
+            pltpu.VMEM((toks, head_dim), F32),
+            pltpu.VMEM((toks, head_dim), F32),
             pltpu.VMEM((2, 2, nz * depth, kv_count * head_dim), BF16),
             pltpu.VMEM((NY, rows, depth * nz // 2), BF16),
             pltpu.VMEM((toks, depth * nz), BF16),
@@ -974,10 +1074,22 @@
             dma((peers,)),
             dma((count - 1,)),
             dma((count - 1,)),
+            dma((8,)),
+            dma((2,)),
         ],
         compiler_params=pltpu.CompilerParams(collective_id=0, has_side_effects=True),
         name="main",
-    )(hidden[0], gain, w, q, cos, sin, out_grad[0], adapt_up[0], adapt_down[0], doc_ids[None])
+    )(
+        hidden[0],
+        gain,
+        w,
+        queries[0],
+        freqs,
+        out_grad[0],
+        adapt_up[0],
+        adapt_down[0],
+        doc_ids[None],
+    )
 
     ceiling = 0.5 * math.sqrt(sections * rank * (local_query + width) * 2)
     return pl.pallas_call(
@@ -988,8 +1100,20 @@
             jax.ShapeDtypeStruct((rank, local_query), F32),
             jax.ShapeDtypeStruct((rank, width), F32),
         ),
-        in_specs=[vmem] * 5,
-        out_specs=[vmem] * 4,
+        in_specs=[hbm] * 5,
+        out_specs=[hbm] * 4,
+        scratch_shapes=[
+            pltpu.VMEM((rows, local_query), BF16),
+            pltpu.VMEM((rank, rows), BF16),
+            pltpu.VMEM((count, chunk, 128), BF16),
+            pltpu.VMEM((count, 8, 128), F32),
+            pltpu.VMEM((rank, width), BF16),
+            pltpu.VMEM((rows, width), BF16),
+            pltpu.VMEM((rank, local_query), F32),
+            pltpu.VMEM((rank, width), F32),
+            dma((6,)),
+            dma((8,)),
+        ],
         name="finish",
     )(att, low, summed, squares, adapt_up[0])
 

time: 116 us -> 106 us (0.914)
  Pallas kernels: 112 us -> 103 us
    pallas_call x1, Pallas kernels: 109 us -> 100 us  [per_device(): pl.pallas_call(lambda *refs: main_kernel(nz, sections, *refs), out_shape=...]
    select_n x1 -> x0, other arithmetic: 1.25 us -> none  [rope_tables(): jnp.where(lane[None, :] < half, -jnp.sin(angles), jnp.sin(angles))]
where the time goes in v3:
time: 106 us
  Pallas kernels  103 us (97%)
  local copies, waits for them, and re-layouts  1.96 us (2%)
    pallas_call x1, Pallas kernels, per_device(): pl.pallas_call(lambda *refs: main_kernel(nz, sections, *refs), out_shape=...  100 us
    pallas_call x1, Pallas kernels, per_device(): pl.pallas_call(lambda *refs: finish_kernel(ceiling, *refs), out_shape=(ja...  2.56 us

profile of v3, /device:TPU:1, one launch (start us, length us, event | category | flops | bytes accessed | tf_op | source)
XLA Modules:
  0.0 106.2 jit_solution(3533369652072848089)
XLA Ops:
  0.6 0.6 maximum_bitcast_fusion.refs_4_
  1.2 1.1 %copy.12 = bf16[2,256,2,128]{3,2,1,0:T(2,128)(2,1)S(1)} copy(bf16[2,256,2,128]{3,0,2,1:T(2,128)(2,1)} %bitcast.20) | data formatting | bytes 524288 | tf_op jit(solution)/shard_map/transpose | solution.py:981
  2.3 0.9 reshape.11.refs_2_
  3.2 100.3 %main.1 = (bf16[128,2048]{1,0:T(8,128)(2,1)}, bf16[16,128]{1,0:T(8,128)(2,1)}, bf16[32,24,128]{2,1,0:T(8,128)(2,1)}, f32[32,8,128]{2,1,0:T(8,128)}) custom-call(bf16[128,4096]{1,0:T(8,128)(2,1)} %bitcast.15, bf16[1,4096]{1,0:T(2,128)(2,1)} %refs_1_.1, bf16[2,256,256]{2,1,0:T(8,128)(2,1)} %reshape.11.refs_2_, bf16[128,16,128]{2,1,0:T(8,128)(2,1)} %bitcast.19, ...), custom_call_target="tpu_custom_call" | custom-call | tf_op jit(solution)/shard_map/main/pallas_call | solution.py:990
  103.5 2.6 %finish.1 = (bf16[128,2048]{1,0:T(8,128)(2,1)}, bf16[128,4096]{1,0:T(8,128)(2,1)}, f32[16,2048]{1,0:T(8,128)}, f32[16,4096]{1,0:T(8,128)}) custom-call(bf16[128,2048]{1,0:T(8,128)(2,1)} %get-tuple-element.12.refs_0_, bf16[16,128]{1,0:T(8,128)(2,1)} %get-tuple-element.13.refs_1_, bf16[32,24,128]{2,1,0:T(8,128)(2,1)} %get-tuple-element.14.refs_2_, ...), custom_call_target="tpu_custom_call" | custom-call | tf_op jit(solution)/shard_map/finish/pallas_call | solution.py:1095
  (1 shorter events, 0.0 us)

commit v4 on v3

--- a/solution.py
+++ b/solution.py
@@ -9,6 +9,7 @@
 
 MESH = pl.DeviceIdType.MESH
 NY = 4
+PIECE = 64
 F32 = jnp.float32
 BF16 = jnp.bfloat16
 
@@ -160,7 +161,9 @@
     q_all,
     bias_ref,
     top,
-    total,
+    s_buf,
+    p_buf,
+    v_ext,
     acc,
     att,
     low_src,
@@ -547,41 +550,52 @@
             allowed = jnp.logical_and(allowed, k_pos <= q_pos)
         bias_ref[...] = jnp.where(allowed, 0.0, -1e30)
 
-        def head(h):
+        for core in range(2):
+            v_ext[:head_dim, core * toks : (core + 1) * toks] = v_all[kb, core]
+
+        tops, shrinks = {}, {}
+
+        def score(h):
             q = q_all[h]
-            scores = [
-                lax.dot_general(
-                    k_all[kb, core], q, (((1,), (1,)), ((), ())), preferred_element_type=F32
+            slot = h % 2
+            peak = None
+            for core in range(2):
+                scores = (
+                    lax.dot_general(
+                        k_all[kb, core], q, (((1,), (1,)), ((), ())), preferred_element_type=F32
+                    )
+                    + bias_ref[core * toks : (core + 1) * toks, :]
                 )
-                + bias_ref[core * toks : (core + 1) * toks, :]
-                for core in range(2)
-            ]
-            peak = jnp.maximum(
-                jnp.max(scores[0], axis=0, keepdims=True), jnp.max(scores[1], axis=0, keepdims=True)
-            )
-            if first:
-                new_top = peak
-            else:
+                s_buf[slot, core] = scores
+                here = jnp.max(scores, axis=0, keepdims=True)
+                peak = here if peak is None else jnp.maximum(peak, here)
+            if not first:
                 old_top = top[h]
-                new_top = jnp.maximum(old_top, peak)
-                shrink = jnp.exp2((old_top - new_top) * factor)
-            weights = [jnp.exp2((s - new_top) * factor) for s in scores]
-            part_sum = jnp.sum(weights[0], axis=0, keepdims=True) + jnp.sum(
-                weights[1], axis=0, keepdims=True
-            )
-            part = jnp.dot(
-                v_all[kb, 0], weights[0].astype(BF16), preferred_element_type=F32
-            ) + jnp.dot(v_all[kb, 1], weights[1].astype(BF16), preferred_element_type=F32)
-            top[h] = new_top
-            if first:
-                total[h] = part_sum
-                acc[h] = part
-            else:
-                total[h] = total[h] * shrink + part_sum
-                acc[h] = acc[h] * shrink + part
-
-        for h in range(heads):
-            head(h)
+                peak = jnp.maximum(old_top, peak)
+                shrinks[h] = jnp.exp2((old_top - peak) * factor)
+            top[h] = peak
+            tops[h] = peak
+
+        def weigh(h):
+            slot = h % 2
+            for core in range(2):
+                for r in range(0, toks, PIECE):
+                    p_buf[slot, core * toks + r : core * toks + r + PIECE, :] = jnp.exp2(
+                        (s_buf[slot, core, r : r + PIECE, :] - tops[h]) * factor
+                    ).astype(BF16)
+
+        def mix(h):
+            slot = h % 2
+            part = jnp.dot(v_ext[...], p_buf[slot], preferred_element_type=F32)[: head_dim + 8]
+            acc[h] = part if first else acc[h] * shrinks[h] + part
+
+        for i in range(heads + 2):
+            if i < heads:
+                score(i)
+            if 0 <= i - 1 < heads:
+                weigh(i - 1)
+            if i >= 2:
+                mix(i - 2)
 
     def await_aside(index, zi):
         for ring in kv_rings:
@@ -600,6 +614,7 @@
 
         lax.fori_loop(0, 2, one, 0)
 
+    v_ext[head_dim:, :] = jnp.ones((16, 2 * toks), BF16)
     await_aside(0, z)
     block(z, True)
     for s in range(1, steps):
@@ -619,7 +634,7 @@
     half_cols = heads * head_dim
     low = None
     for h in range(heads):
-        out = acc[h] / total[h]
+        out = acc[h, :head_dim, :] / acc[h, head_dim : head_dim + 1, :]
         factor_cols = down_buf[
             home, :, pl.ds(pl.multiple_of((y % 2) * half_cols + h * head_dim, head_dim), head_dim)
         ]
@@ -1027,8 +1042,10 @@
             pltpu.VMEM((group, toks, head_dim), BF16),
             pltpu.VMEM((2 * toks, toks), F32),
             pltpu.VMEM((group, 1, toks), F32),
-            pltpu.VMEM((group, 1, toks), F32),
-            pltpu.VMEM((group, head_dim, toks), F32),
+            pltpu.VMEM((2, 2, toks, toks), F32),
+            pltpu.VMEM((2, 2 * toks, toks), BF16),
+            pltpu.VMEM((head_dim + 16, 2 * toks), BF16),
+            pltpu.VMEM((group, head_dim + 8, toks), F32),
             pltpu.VMEM((toks, group * head_dim), BF16),
             pltpu.VMEM((2, rank, rows), F32),
             pltpu.VMEM((NY, rank, rows), F32),

time: 106 us -> 96.1 us (0.907)
  Pallas kernels: 103 us -> 92.5 us
    pallas_call x1, Pallas kernels: 100 us -> 90 us  [per_device(): pl.pallas_call(lambda *refs: main_kernel(nz, sections, *refs), out_shape=...]
where the time goes in v4:
time: 96.1 us; the launch traced here: 95.9 us
  Pallas kernels  92.5 us (96%)
  local copies, waits for them, and re-layouts  1.96 us (2%)
    pallas_call x1, Pallas kernels, per_device(): pl.pallas_call(lambda *refs: main_kernel(nz, sections, *refs), out_shape=...  90 us
    pallas_call x1, Pallas kernels, per_device(): pl.pallas_call(lambda *refs: finish_kernel(ceiling, *refs), out_shape=(ja...  2.56 us

profile of v4, /device:TPU:1, one launch (start us, length us, event | category | flops | bytes accessed | tf_op | source)
XLA Modules:
  0.0 95.9 jit_solution(16180224305760464402)
XLA Ops:
  0.6 0.6 maximum_bitcast_fusion.refs_4_
  1.2 1.1 %copy.12 = bf16[2,256,2,128]{3,2,1,0:T(2,128)(2,1)S(1)} copy(bf16[2,256,2,128]{3,0,2,1:T(2,128)(2,1)} %bitcast.20) | data formatting | bytes 524288 | tf_op jit(solution)/shard_map/transpose | solution.py:996
  2.3 0.9 reshape.11.refs_2_
  3.2 90.0 %main.1 = (bf16[128,2048]{1,0:T(8,128)(2,1)}, bf16[16,128]{1,0:T(8,128)(2,1)}, bf16[32,24,128]{2,1,0:T(8,128)(2,1)}, f32[32,8,128]{2,1,0:T(8,128)}) custom-call(bf16[128,4096]{1,0:T(8,128)(2,1)} %bitcast.15, bf16[1,4096]{1,0:T(2,128)(2,1)} %refs_1_.1, bf16[2,256,256]{2,1,0:T(8,128)(2,1)} %reshape.11.refs_2_, bf16[128,16,128]{2,1,0:T(8,128)(2,1)} %bitcast.19, ...), custom_call_target="tpu_custom_call" | custom-call | tf_op jit(solution)/shard_map/main/pallas_call | solution.py:1005
  93.2 2.6 %finish.1 = (bf16[128,2048]{1,0:T(8,128)(2,1)}, bf16[128,4096]{1,0:T(8,128)(2,1)}, f32[16,2048]{1,0:T(8,128)}, f32[16,4096]{1,0:T(8,128)}) custom-call(bf16[128,2048]{1,0:T(8,128)(2,1)} %get-tuple-element.12.refs_0_, bf16[16,128]{1,0:T(8,128)(2,1)} %get-tuple-element.13.refs_1_, bf16[32,24,128]{2,1,0:T(8,128)(2,1)} %get-tuple-element.14.refs_2_, ...), custom_call_target="tpu_custom_call" | custom-call | tf_op jit(solution)/shard_map/finish/pallas_call | solution.py:1112
  (1 shorter events, 0.0 us)

commit v5 on v4

--- a/solution.py
+++ b/solution.py
@@ -2,6 +2,7 @@
 
 import jax
 import jax.numpy as jnp
+import numpy as np
 from jax import lax
 from jax.experimental import pallas as pl
 from jax.experimental.pallas import tpu as pltpu
@@ -121,17 +122,17 @@
     sections,
     hid_hbm,
     gain_ref,
-    w_ref,
+    w_hbm,
     q_hbm,
     freq_ref,
     grad_hbm,
     up_hbm,
     down_hbm,
     doc_ref,
-    att_out,
+    att_hbm,
     low_out,
     all_buf,
-    sq_all,
+    norm_out,
     hid_ref,
     q_raw,
     q_ref,
@@ -140,6 +141,8 @@
     down_ref,
     cos_ref,
     sin_ref,
+    w_raw,
+    w_wide,
     w_buf,
     normed,
     x_buf,
@@ -174,6 +177,8 @@
     dred_in,
     sq_src,
     sq_in,
+    sq_all,
+    att_out,
     w_send,
     w_recv,
     ws_send,
@@ -216,7 +221,7 @@
     z, y, t = position()
     section = lax.axis_index("section")
     rows, width = hid_ref.shape
-    depth = w_ref.shape[1]
+    depth = w_buf.shape[2] // nz
     cols = depth * nz // 2
     head_dim = k_all.shape[-1]
     heads = q_all.shape[0]
@@ -257,8 +262,18 @@
             ((q_hbm, q_raw), (grad_hbm, grad_ref), (up_hbm, up_ref), (down_hbm, down_ref))
         )
     ]
+    w_load = pltpu.make_async_copy(w_hbm, w_raw, own_sem.at[0])
+    w_load.start()
     for load in hid_loads:
         load.start()
+    own_rows = pl.ds(pl.multiple_of(z * depth, depth), depth)
+    w_load.wait()
+    w_wide[...] = w_raw[...].astype(F32)
+    for p in (0, 1):
+        for h in range(2):
+            w_buf[p, t, own_rows, h * head_dim : (h + 1) * head_dim] = w_wide[
+                pl.ds(2 * h + p, depth, stride=4), :
+            ].astype(BF16)
     pl.semaphore_wait(barrier, 2 + 2 * NY - 1 + 2 * (sections - 1))
 
     def w_block(p):
@@ -285,13 +300,9 @@
         for p, buf in ((0, k_all), (1, v_all))
     ]
 
-    w_rings[0].start(w_ref.at[0])
-    w_rings[1].start(w_ref.at[1])
-    own_rows = pl.ds(pl.multiple_of(z * depth, depth), depth)
-    own_loads = [
-        pltpu.make_async_copy(w_ref.at[p], w_buf.at[p, t, own_rows], own_sem.at[p]) for p in (0, 1)
-    ]
-    for load in late_loads + own_loads:
+    w_rings[0].start()
+    w_rings[1].start()
+    for load in late_loads:
         load.start()
 
     doc_own = doc_in.at[0]
@@ -502,8 +513,6 @@
         return (v * cos_ref[...] + pltpu.roll(v, head_dim // 2, 1) * sin_ref[...]).astype(BF16)
 
     x_wait()
-    for load in own_loads:
-        load.wait()
     w_rings[0].final()
     w_rings[0].wait_sibling()
     project(0, k_part)
@@ -533,6 +542,18 @@
         axis=1,
     )
 
+    q_pos = (z * 2 + t) * toks + lax.broadcasted_iota(jnp.int32, (keys, toks), 1)
+    k_pos = lax.broadcasted_iota(jnp.int32, (keys, toks), 0)
+
+    def mask(kb, carry):
+        turned = jnp.transpose(doc_all[kb].astype(F32))
+        k_doc = jnp.concatenate([turned[:, j : j + 1] for j in range(NY)], axis=0)
+        allowed = jnp.logical_and(k_doc == q_doc, k_pos + kb * keys <= q_pos)
+        bias_ref[kb] = jnp.where(allowed, 0.0, -1e30)
+        return carry
+
+    lax.fori_loop(0, nz, mask, 0)
+
     k_all[z, t] = rope(collect(0))
     kv_rings[0].start()
     v_all[z, t] = jnp.transpose(collect(1)).astype(BF16)
@@ -541,15 +562,6 @@
     factor = head_dim ** (-0.5) * math.log2(math.e)
 
     def block(kb, first):
-        turned = jnp.transpose(doc_all[kb].astype(F32))
-        k_doc = jnp.concatenate([turned[:, j : j + 1] for j in range(NY)], axis=0)
-        allowed = k_doc == q_doc
-        if first:
-            q_pos = t * toks + lax.broadcasted_iota(jnp.int32, (keys, toks), 1)
-            k_pos = lax.broadcasted_iota(jnp.int32, (keys, toks), 0)
-            allowed = jnp.logical_and(allowed, k_pos <= q_pos)
-        bias_ref[...] = jnp.where(allowed, 0.0, -1e30)
-
         for core in range(2):
             v_ext[:head_dim, core * toks : (core + 1) * toks] = v_all[kb, core]
 
@@ -564,7 +576,7 @@
                     lax.dot_general(
                         k_all[kb, core], q, (((1,), (1,)), ((), ())), preferred_element_type=F32
                     )
-                    + bias_ref[core * toks : (core + 1) * toks, :]
+                    + bias_ref[kb, core * toks : (core + 1) * toks, :]
                 )
                 s_buf[slot, core] = scores
                 here = jnp.max(scores, axis=0, keepdims=True)
@@ -894,12 +906,19 @@
             dest = att_dest(kvl)
             remote(dest, dest, att_send.at[0], att_recv.at[kvl], **sibling).wait_recv()
 
+    att_store = pltpu.make_async_copy(att_out, att_hbm, own_sem.at[1])
+    att_store.start()
     all_wait()
     all_drain()
     for i in range(len(peers)):
         sq_copy(i).wait_send()
     sqa_wait()
     sqa_drain()
+    norm = sq_all[0]
+    for c in range(1, count):
+        norm = norm + sq_all[c]
+    norm_out[...] = norm
+    att_store.wait()
 
 
 def finish_kernel(
@@ -965,10 +984,7 @@
         put(att_ref.at[half], att_out.at[half])
     ins[2].wait()
     ins[3].wait()
-    norm = sq_ref[0]
-    for c in range(1, count):
-        norm = norm + sq_ref[c]
-    clip = jnp.minimum(1.0, ceiling / (jnp.sqrt(norm[0:1, 0:1]) + 1e-06))
+    clip = jnp.minimum(1.0, ceiling / (jnp.sqrt(sq_ref[0:1, 0:1]) + 1e-06))
     for c in range(count):
         r0 = 8 * (c // blocks)
         c0 = 128 * (c % blocks)
@@ -991,9 +1007,9 @@
     rank, local_query = adapt_down.shape[1:]
     toks = 2 * rows
     half = head_dim // 2
-    freqs = 1000000.0 ** (-jnp.arange(half, dtype=F32) * 2.0 / head_dim)
-    freqs = jnp.concatenate([freqs, freqs])[None]
-    w = key_value_weight[0].transpose(2, 0, 1, 3).reshape(2, depth, kv_count * head_dim)
+    freqs = (1000000.0 ** (-np.arange(half) * 2.0 / head_dim)).astype(np.float32)
+    freqs = jnp.asarray(np.concatenate([freqs, freqs])[None])
+    w = key_value_weight.reshape(depth * kv_count * 2, head_dim)
 
     vmem = pl.BlockSpec(memory_space=pltpu.VMEM)
     hbm = pl.BlockSpec(memory_space=pl.ANY)
@@ -1008,10 +1024,10 @@
             jax.ShapeDtypeStruct((rows, local_query), BF16),
             jax.ShapeDtypeStruct((rank, rows), BF16),
             jax.ShapeDtypeStruct((count, chunk, 128), BF16),
-            jax.ShapeDtypeStruct((count, 8, 128), F32),
+            jax.ShapeDtypeStruct((8, 128), F32),
         ),
         in_specs=[hbm, vmem, hbm, hbm, vmem, hbm, hbm, hbm, vmem],
-        out_specs=[vmem] * 4,
+        out_specs=[hbm, vmem, vmem, vmem],
         scratch_shapes=[
             pltpu.VMEM((rows, width), BF16),
             pltpu.VMEM((rows, heads, head_dim), BF16),
@@ -1021,6 +1037,8 @@
             pltpu.VMEM((rank, local_query), BF16),
             pltpu.VMEM((toks, head_dim), F32),
             pltpu.VMEM((toks, head_dim), F32),
+            pltpu.VMEM((depth * kv_count * 2, head_dim), BF16),
+            pltpu.VMEM((depth * kv_count * 2, head_dim), F32),
             pltpu.VMEM((2, 2, nz * depth, kv_count * head_dim), BF16),
             pltpu.VMEM((NY, rows, depth * nz // 2), BF16),
             pltpu.VMEM((toks, depth * nz), BF16),
@@ -1040,7 +1058,7 @@
             pltpu.VMEM((nz, 2, toks, head_dim), BF16),
             pltpu.VMEM((nz, 2, head_dim, toks), BF16),
             pltpu.VMEM((group, toks, head_dim), BF16),
-            pltpu.VMEM((2 * toks, toks), F32),
+            pltpu.VMEM((nz, 2 * toks, toks), F32),
             pltpu.VMEM((group, 1, toks), F32),
             pltpu.VMEM((2, 2, toks, toks), F32),
             pltpu.VMEM((2, 2 * toks, toks), BF16),
@@ -1055,6 +1073,8 @@
             pltpu.VMEM((2 * nz, 8, 128), BF16),
             pltpu.VMEM((8, 128), F32),
             pltpu.VMEM((peers, 8, 128), F32),
+            pltpu.VMEM((count, 8, 128), F32),
+            pltpu.VMEM((rows, local_query), BF16),
             dma((2, 2, steps)),
             dma((2, 2, steps)),
             dma((2, nz)),
@@ -1123,7 +1143,7 @@
             pltpu.VMEM((rows, local_query), BF16),
             pltpu.VMEM((rank, rows), BF16),
             pltpu.VMEM((count, chunk, 128), BF16),
-            pltpu.VMEM((count, 8, 128), F32),
+            pltpu.VMEM((8, 128), F32),
             pltpu.VMEM((rank, width), BF16),
             pltpu.VMEM((rows, width), BF16),
             pltpu.VMEM((rank, local_query), F32),

time: 96.1 us -> 93.5 us (0.973)
  local copies, waits for them, and re-layouts: 1.96 us -> 0 us
    transpose x1 -> x0, local copies, waits for them, and re-layouts: 1.09 us -> none  [per_device(): key_value_weight[0].transpose(2, 0, 1, 3)]
where the time goes in v5:
time: 93.5 us; the launch traced here: 93.3 us
  Pallas kernels  92.5 us (99%)
    pallas_call x1, Pallas kernels, per_device(): pl.pallas_call(lambda *refs: main_kernel(nz, sections, *refs), out_shape=...  90 us
    pallas_call x1, Pallas kernels, per_device(): pl.pallas_call(lambda *refs: finish_kernel(ceiling, *refs), out_shape=(ja...  2.56 us

profile of v5, /device:TPU:1, one launch (start us, length us, event | category | flops | bytes accessed | tf_op | source)
XLA Modules:
  0.0 93.3 jit_solution(14399159494459717079)
XLA Ops:
  0.6 90.0 %main.1 = (bf16[128,2048]{1,0:T(8,128)(2,1)}, bf16[16,128]{1,0:T(8,128)(2,1)}, bf16[32,24,128]{2,1,0:T(8,128)(2,1)}, f32[8,128]{1,0:T(8,128)}) custom-call(bf16[128,4096]{1,0:T(8,128)(2,1)} %bitcast.11, bf16[1,4096]{1,0:T(2,128)(2,1)} %refs_1_.1, bf16[1024,128]{1,0:T(8,128)(2,1)} %bitcast.16, bf16[128,16,128]{2,1,0:T(8,128)(2,1)} %bitcast.15, ...), custom_call_target="tpu_custom_call" | custom-call | tf_op jit(solution)/shard_map/main/pallas_call | solution.py:1021
  90.6 2.6 %finish.1 = (bf16[128,2048]{1,0:T(8,128)(2,1)}, bf16[128,4096]{1,0:T(8,128)(2,1)}, f32[16,2048]{1,0:T(8,128)}, f32[16,4096]{1,0:T(8,128)}) custom-call(bf16[128,2048]{1,0:T(8,128)(2,1)} %get-tuple-element.12.refs_0_, bf16[16,128]{1,0:T(8,128)(2,1)} %get-tuple-element.13.refs_1_, bf16[32,24,128]{2,1,0:T(8,128)(2,1)} %get-tuple-element.14.refs_2_, ...), custom_call_target="tpu_custom_call" | custom-call | tf_op jit(solution)/shard_map/finish/pallas_call | solution.py:1132

commit v6 on v5

--- a/solution.py
+++ b/solution.py
@@ -32,9 +32,9 @@
 
 
 class Ring:
-    def __init__(self, nz, block, half, send, recv, sib_send=None, sib_recv=None):
+    def __init__(self, nz, half, send, recv, sib_send, sib_recv):
         self.nz, self.steps = nz, nz // 2
-        self.block, self.half = block, half
+        self.half = half
         self.send, self.recv = send, recv
         self.sib_send, self.sib_recv = sib_send, sib_recv
         self.z, self.y, self.t = position()
@@ -46,53 +46,51 @@
         z = (self.z + 1) % self.nz if d == 0 else (self.z + self.nz - 1) % self.nz
         return dict(ctx=z * NY + self.y, tp=self.t)
 
-    def piece(self, zi, d, s):
-        return self.half(zi, d, self.t) if s == self.steps else self.block(zi, self.t)
-
-    def hop(self, d, s, src=None):
-        piece = self.piece(self.origin(d, s - 1), d, s)
-        return remote(
-            piece if src is None else src,
+    def carried(self, d, s):
+        return (0, 1) if s < self.steps else (d,)
+
+    def copy(self, d, s, zi, i):
+        piece = self.half(zi, i, self.t)
+        return remote(
             piece,
-            self.send.at[d, s - 1],
-            self.recv.at[d, s - 1],
+            piece,
+            self.send.at[d, s - 1, i],
+            self.recv.at[d, s - 1, i],
             **self.neighbour(d),
         )
 
-    def arrival(self, d, s):
-        piece = self.piece(self.origin(d, s), d, s)
-        return remote(
-            piece, piece, self.send.at[d, s - 1], self.recv.at[d, s - 1], **self.neighbour(d)
-        )
-
-    def aside(self, index, zi, core, src=None):
-        piece = self.block(zi, core)
-        return remote(
-            piece if src is None else src,
-            piece,
-            self.sib_send.at[index],
-            self.sib_recv.at[index],
-            tp=1 - self.t,
-        )
-
-    def start(self, src=None):
-        for d in (0, 1):
-            self.hop(d, 1, src).start()
-        if self.sib_send is not None:
-            self.aside(0, self.z, self.t, src).start()
+    def hop(self, d, s, i):
+        return self.copy(d, s, self.origin(d, s - 1), i)
+
+    def arrival(self, d, s, i):
+        return self.copy(d, s, self.origin(d, s), i)
+
+    def aside(self, index, zi, core, i):
+        piece = self.half(zi, i, core)
+        return remote(
+            piece, piece, self.sib_send.at[index, i], self.sib_recv.at[index, i], tp=1 - self.t
+        )
+
+    def start(self):
+        for i in (0, 1):
+            for d in (0, 1):
+                if i in self.carried(d, 1):
+                    self.hop(d, 1, i).start()
+        for i in (0, 1):
+            self.aside(0, self.z, self.t, i).start()
 
     def step(self, s):
-        for d in (0, 1):
-            self.arrival(d, s).wait_recv()
-            self.hop(d, s + 1).start()
-            if self.sib_send is not None:
-                self.aside(2 * s - 1 + d, self.origin(d, s), self.t).start()
+        for i in (0, 1):
+            for d in (0, 1):
+                self.arrival(d, s, i).wait_recv()
+                if i in self.carried(d, s + 1):
+                    self.hop(d, s + 1, i).start()
+                self.aside(2 * s - 1 + d, self.origin(d, s), self.t, i).start()
 
     def final(self):
         for d in (0, 1):
-            self.arrival(d, self.steps).wait_recv()
-        if self.sib_send is not None:
-            self.aside(self.nz - 1, self.origin(0, self.steps), self.t).start()
+            self.arrival(d, self.steps, d).wait_recv()
+            self.aside(self.nz - 1, self.origin(0, self.steps), self.t, d).start()
 
     def asides(self):
         yield 0, self.z
@@ -102,7 +100,8 @@
         yield self.nz - 1, self.origin(0, self.steps)
 
     def wait_aside(self, index, zi):
-        self.aside(index, zi, 1 - self.t).wait_recv()
+        for i in (0, 1):
+            self.aside(index, zi, 1 - self.t, i).wait_recv()
 
     def wait_sibling(self):
         for index, zi in self.asides():
@@ -111,10 +110,11 @@
     def drain(self):
         for d in (0, 1):
             for s in range(1, self.steps + 1):
-                self.hop(d, s).wait_send()
-        if self.sib_send is not None:
-            for index, zi in self.asides():
-                self.aside(index, zi, self.t).wait_send()
+                for i in self.carried(d, s):
+                    self.hop(d, s, i).wait_send()
+        for index, zi in self.asides():
+            for i in (0, 1):
+                self.aside(index, zi, self.t, i).wait_send()
 
 
 def main_kernel(
@@ -276,32 +276,25 @@
             ].astype(BF16)
     pl.semaphore_wait(barrier, 2 + 2 * NY - 1 + 2 * (sections - 1))
 
-    def w_block(p):
-        return lambda zi, core: w_buf.at[p, core, pl.ds(pl.multiple_of(zi * depth, depth), depth)]
-
     def w_half(p):
         return lambda zi, h, core: w_buf.at[
             p, core, pl.ds(pl.multiple_of(zi * depth + h * (depth // 2), depth // 2), depth // 2)
         ]
 
-    def kv_block(buf):
-        return lambda zi, core: buf.at[zi, core]
-
     def kv_half(buf):
         size = buf.shape[2] // 2
         return lambda zi, h, core: buf.at[zi, core, pl.ds(h * size, size)]
 
     w_rings = [
-        Ring(nz, w_block(p), w_half(p), w_send.at[p], w_recv.at[p], ws_send.at[p], ws_recv.at[p])
+        Ring(nz, w_half(p), w_send.at[p], w_recv.at[p], ws_send.at[p], ws_recv.at[p])
         for p in (0, 1)
     ]
     kv_rings = [
-        Ring(nz, kv_block(buf), kv_half(buf), kv_send.at[p], kv_recv.at[p], kvs_send.at[p], kvs_recv.at[p])
+        Ring(nz, kv_half(buf), kv_send.at[p], kv_recv.at[p], kvs_send.at[p], kvs_recv.at[p])
         for p, buf in ((0, k_all), (1, v_all))
     ]
 
     w_rings[0].start()
-    w_rings[1].start()
     for load in late_loads:
         load.start()
 
@@ -455,7 +448,8 @@
 
     for s in range(1, steps):
         w_rings[0].step(s)
-        w_rings[1].step(s)
+        if s == max(1, steps - 2):
+            w_rings[1].start()
         doc_step(s)
         if s == 2:
             lane = lax.broadcasted_iota(jnp.int32, cos_ref.shape, 1)
@@ -484,7 +478,10 @@
                     remote(dest, dest, x_send.at[0], x_recv.at[b, core], **sibling).wait_recv()
 
     def project(p, part):
-        for core in range(2):
+        w_rings[p].final()
+        for core in (t, 1 - t):
+            if core is not t:
+                w_rings[p].wait_sibling()
             partial = jnp.dot(x_buf[...], w_buf[p, core], preferred_element_type=F32)
             for hl in range(2):
                 part[2 * core + hl] = partial[:, hl * head_dim : (hl + 1) * head_dim].astype(part.dtype)
@@ -512,14 +509,13 @@
     def rope(v):
         return (v * cos_ref[...] + pltpu.roll(v, head_dim // 2, 1) * sin_ref[...]).astype(BF16)
 
+    w_rings[1].step(1)
     x_wait()
-    w_rings[0].final()
-    w_rings[0].wait_sibling()
     project(0, k_part)
     for oy in range(1, NY):
         scatter_copy(0, oy).start()
-    w_rings[1].final()
-    w_rings[1].wait_sibling()
+    for s in range(2, steps):
+        w_rings[1].step(s)
     project(1, v_part)
     for oy in range(1, NY):
         scatter_copy(1, oy).start()
@@ -1075,14 +1071,14 @@
             pltpu.VMEM((peers, 8, 128), F32),
             pltpu.VMEM((count, 8, 128), F32),
             pltpu.VMEM((rows, local_query), BF16),
-            dma((2, 2, steps)),
-            dma((2, 2, steps)),
-            dma((2, nz)),
-            dma((2, nz)),
-            dma((2, 2, steps)),
-            dma((2, 2, steps)),
-            dma((2, nz)),
-            dma((2, nz)),
+            dma((2, 2, steps, 2)),
+            dma((2, 2, steps, 2)),
+            dma((2, nz, 2)),
+            dma((2, nz, 2)),
+            dma((2, 2, steps, 2)),
+            dma((2, 2, steps, 2)),
+            dma((2, nz, 2)),
+            dma((2, nz, 2)),
             dma((2, steps)),
             dma((2, steps)),
             dma((NY,)),

time: 93.5 us -> 97.9 us (1.047)
  Pallas kernels: 92.5 us -> 96.9 us
    pallas_call x1, Pallas kernels: 90 us -> 94.3 us  [per_device(): pl.pallas_call(lambda *refs: main_kernel(nz, sections, *refs), out_shape=...]
where the time goes in v6:
time: 97.9 us; the launch traced here: 97.7 us
  Pallas kernels  96.9 us (99%)
    pallas_call x1, Pallas kernels, per_device(): pl.pallas_call(lambda *refs: main_kernel(nz, sections, *refs), out_shape=...  94.3 us
    pallas_call x1, Pallas kernels, per_device(): pl.pallas_call(lambda *refs: finish_kernel(ceiling, *refs), out_shape=(ja...  2.56 us

profile of v6, /device:TPU:1, one launch (start us, length us, event | category | flops | bytes accessed | tf_op | source)
XLA Modules:
  0.0 97.7 jit_solution(1432420492068319494)
XLA Ops:
  0.6 94.3 %main.1 = (bf16[128,2048]{1,0:T(8,128)(2,1)}, bf16[16,128]{1,0:T(8,128)(2,1)}, bf16[32,24,128]{2,1,0:T(8,128)(2,1)}, f32[8,128]{1,0:T(8,128)}) custom-call(bf16[128,4096]{1,0:T(8,128)(2,1)} %bitcast.11, bf16[1,4096]{1,0:T(2,128)(2,1)} %refs_1_.1, bf16[1024,128]{1,0:T(8,128)(2,1)} %bitcast.16, bf16[128,16,128]{2,1,0:T(8,128)(2,1)} %bitcast.15, ...), custom_call_target="tpu_custom_call" | custom-call | tf_op jit(solution)/shard_map/main/pallas_call | solution.py:1017
  95.0 2.6 %finish.1 = (bf16[128,2048]{1,0:T(8,128)(2,1)}, bf16[128,4096]{1,0:T(8,128)(2,1)}, f32[16,2048]{1,0:T(8,128)}, f32[16,4096]{1,0:T(8,128)}) custom-call(bf16[128,2048]{1,0:T(8,128)(2,1)} %get-tuple-element.12.refs_0_, bf16[16,128]{1,0:T(8,128)(2,1)} %get-tuple-element.13.refs_1_, bf16[32,24,128]{2,1,0:T(8,128)(2,1)} %get-tuple-element.14.refs_2_, ...), custom_call_target="tpu_custom_call" | custom-call | tf_op jit(solution)/shard_map/finish/pallas_call | solution.py:1128

commit v7 on v5

--- a/solution.py
+++ b/solution.py
@@ -724,37 +724,6 @@
 
     lax.fori_loop(0, 2 * heads, dred_start, 0)
 
-    for src_y in range(NY):
-
-        @pl.when(jnp.logical_or(src_y != y, home != t))
-        def _():
-            remote(
-                low_in.at[src_y], low_in.at[src_y], low_send.at[0, 0], low_recv.at[src_y], **sibling
-            ).wait_recv()
-
-    low = low_in[0]
-    for src_y in range(1, NY):
-        low = low + low_in[src_y]
-    low = low.astype(BF16)
-    low_out[...] = low
-
-    for c in range(count):
-        red_src[c] = jnp.dot(
-            low, grad_ref[:, c * 128 : (c + 1) * 128], preferred_element_type=F32
-        ).astype(BF16)
-
-    def red_copy(o):
-        to = (me + o) % count
-        return remote(
-            red_src.at[to], red_in.at[o - 1], red_send.at[o - 1], red_recv.at[o - 1], ctx=to
-        )
-
-    def red_start(o, carry):
-        red_copy(o).start()
-        return carry
-
-    lax.fori_loop(1, count, red_start, 0)
-
     def att_dest(kvl):
         return att_out.at[:, pl.ds(pl.multiple_of(kvl * half_cols, half_cols), half_cols)]
 
@@ -779,6 +748,37 @@
             att_out[:, pl.ds(pl.multiple_of((y % 2) * half_cols, half_cols), half_cols)] = att[
                 b * rows : (b + 1) * rows
             ]
+
+    for src_y in range(NY):
+
+        @pl.when(jnp.logical_or(src_y != y, home != t))
+        def _():
+            remote(
+                low_in.at[src_y], low_in.at[src_y], low_send.at[0, 0], low_recv.at[src_y], **sibling
+            ).wait_recv()
+
+    low = low_in[0]
+    for src_y in range(1, NY):
+        low = low + low_in[src_y]
+    low = low.astype(BF16)
+    low_out[...] = low
+
+    for c in range(count):
+        red_src[c] = jnp.dot(
+            low, grad_ref[:, c * 128 : (c + 1) * 128], preferred_element_type=F32
+        ).astype(BF16)
+
+    def red_copy(o):
+        to = (me + o) % count
+        return remote(
+            red_src.at[to], red_in.at[o - 1], red_send.at[o - 1], red_recv.at[o - 1], ctx=to
+        )
+
+    def red_start(o, carry):
+        red_copy(o).start()
+        return carry
+
+    lax.fori_loop(1, count, red_start, 0)
 
     down_y = 2 * t + (me % blocks) // heads
 

time: 93.5 us -> 93.9 us (level)
  no operation moved by 1% of the time
where the time goes in v7:
time: 93.9 us; the launch traced here: 93.7 us
  Pallas kernels  92.9 us (99%)
    pallas_call x1, Pallas kernels, per_device(): pl.pallas_call(lambda *refs: main_kernel(nz, sections, *refs), out_shape=...  90.4 us
    pallas_call x1, Pallas kernels, per_device(): pl.pallas_call(lambda *refs: finish_kernel(ceiling, *refs), out_shape=(ja...  2.56 us

profile of v7, /device:TPU:1, one launch (start us, length us, event | category | flops | bytes accessed | tf_op | source)
XLA Modules:
  0.0 93.7 jit_solution(13816812390837099453)
XLA Ops:
  0.6 90.4 %main.1 = (bf16[128,2048]{1,0:T(8,128)(2,1)}, bf16[16,128]{1,0:T(8,128)(2,1)}, bf16[32,24,128]{2,1,0:T(8,128)(2,1)}, f32[8,128]{1,0:T(8,128)}) custom-call(bf16[128,4096]{1,0:T(8,128)(2,1)} %bitcast.11, bf16[1,4096]{1,0:T(2,128)(2,1)} %refs_1_.1, bf16[1024,128]{1,0:T(8,128)(2,1)} %bitcast.16, bf16[128,16,128]{2,1,0:T(8,128)(2,1)} %bitcast.15, ...), custom_call_target="tpu_custom_call" | custom-call | tf_op jit(solution)/shard_map/main/pallas_call | solution.py:1021
  91.0 2.6 %finish.1 = (bf16[128,2048]{1,0:T(8,128)(2,1)}, bf16[128,4096]{1,0:T(8,128)(2,1)}, f32[16,2048]{1,0:T(8,128)}, f32[16,4096]{1,0:T(8,128)}) custom-call(bf16[128,2048]{1,0:T(8,128)(2,1)} %get-tuple-element.12.refs_0_, bf16[16,128]{1,0:T(8,128)(2,1)} %get-tuple-element.13.refs_1_, bf16[32,24,128]{2,1,0:T(8,128)(2,1)} %get-tuple-element.14.refs_2_, ...), custom_call_target="tpu_custom_call" | custom-call | tf_op jit(solution)/shard_map/finish/pallas_call | solution.py:1132
